TPU v7x, 32 devices: a whole 2x2x4 slice. The times are simulated.
32 devices in a mesh: slab: 4 (over x, core), grp: 8 (over z, y).
Axes of the slice: x: 2, y: 2, z: 4, core: 2. Of those that a mesh axis runs over, the one named last changes fastest.
Arguments:
- raw_frames: bfloat16 [256, 48, 10752], P('grp', 'slab'), may hold values from -700 to 700
- mask_index: int32 [57344], P(('slab', 'grp')), may hold values from 0 to 516095, as said below
- subspace: bfloat16 [1200, 57344], P(None, ('slab', 'grp')), may hold values from -6 to 6
- rotation: bfloat16 [1456, 1200], replicated, may hold values from -0.15625 to 0.15625
Outputs:
- gram: float32 [1456, 1456], P('grp')
- new_subspace: bfloat16 [1200, 57344], P(None, ('slab', 'grp'))
Inputs may be any that keep to these rules, and one draw needn't show every extreme that they name: `mask_index`: entries are distinct flat grid positions that come in runs of 128 consecutive positions, each run starting at a multiple of 128; the 14336 entries of aligned block s lie in z planes s * 12 to (s + 1) * 12 - 1 and rise within the block; the first 3584 of a block lie in its lowest 3 planes, the last 3584 in its highest 3 planes, the others in the planes between.
All inputs are finite; a program needn't handle non-finite values.
Results may differ from a plain program's by a relative error of at most 0.006.
Values may be sent and summed in bfloat16 or wider, within the bound.
A program may use at most 192 MiB of HBM per device.

v0:
```python
import math

import jax
import jax.numpy as jnp
from jax import lax
from jax.sharding import PartitionSpec as P

NX = 96
RUN = 128
RAD = 3
K = 1200


smooth_sigma = 1.0617
epsilon = 1e-06


def padded_2(cells, sides, width):
    for axis, dim in sides:
        count = lax.axis_size(axis)
        ends = count - 1
        head = lax.slice_in_dim(cells, 0, width, axis=dim)
        tail = lax.slice_in_dim(cells, cells.shape[dim] - width, cells.shape[dim], axis=dim)
        cells = jnp.concatenate(
            [
                lax.ppermute(tail, axis, [(i, (i + 1) % count) for i in range(ends)]),
                cells,
                lax.ppermute(head, axis, [((i + 1) % count, i) for i in range(ends)]),
            ],
            axis=dim,
        )
    return cells


def tap_weights():
    unscaled = [
        math.exp(-offset * offset / (2.0 * smooth_sigma * smooth_sigma))
        for offset in range(-RAD, RAD + 1)
    ]
    summed = sum(unscaled)
    return [weight / summed for weight in unscaled]


def along_rows(volume):
    weights = tap_weights()
    extent = volume.shape[-1]
    column = lax.broadcasted_iota(jnp.int32, (extent,), 0) % NX
    padded = jnp.pad(volume, [(0, 0)] * (volume.ndim - 1) + [(RAD, RAD)])
    summed = jnp.zeros(volume.shape, jnp.float32)
    for offset in range(-RAD, RAD + 1):
        shifted = lax.slice_in_dim(
            padded, RAD + offset, RAD + offset + extent, axis=volume.ndim - 1
        )
        inside = (column + offset >= 0) & (column + offset < NX)
        summed = summed + weights[offset + RAD] * jnp.where(inside, shifted, 0.0)
    return summed


def along_columns(volume):
    weights = tap_weights()
    extent = volume.shape[-1]
    reach_cells = RAD * NX
    padded = jnp.pad(volume, [(0, 0)] * (volume.ndim - 1) + [(reach_cells, reach_cells)])
    summed = jnp.zeros(volume.shape, jnp.float32)
    for offset in range(-RAD, RAD + 1):
        begin = reach_cells + offset * NX
        shifted = lax.slice_in_dim(padded, begin, begin + extent, axis=volume.ndim - 1)
        summed = summed + weights[offset + RAD] * shifted
    return summed


def along_depth(padded, slab_depth):
    weights = tap_weights()
    summed = None
    for offset in range(-RAD, RAD + 1):
        shifted = lax.slice_in_dim(
            padded, RAD + offset, RAD + offset + slab_depth, axis=padded.ndim - 2
        )
        term = weights[offset + RAD] * shifted
        summed = term if summed is None else summed + term
    return summed


def pick_columns(matrix, wanted):
    row_total = matrix.shape[0]
    blocked = matrix.reshape(row_total, matrix.shape[1] // RUN, RUN)
    run_starts = wanted.reshape(-1, RUN)[:, 0] // RUN
    picked_runs = jnp.take(blocked, run_starts, axis=1)
    return picked_runs.reshape(row_total, wanted.shape[0])


def body(raw_frames, mask_index, subspace, rotation):
    frames_here = raw_frames.shape[0]
    slab_depth = raw_frames.shape[1]
    extent = raw_frames.shape[2]
    per_device = subspace.shape[1]
    group_count = lax.axis_size("grp")
    masked = per_device * lax.axis_size("slab") * group_count
    positions = lax.all_gather(mask_index, "grp", axis=0, tiled=True) - lax.axis_index("slab") * (
        slab_depth * extent
    )
    padded = padded_2(raw_frames, (("slab", 1),), RAD)
    planar = along_columns(along_rows(padded.astype(jnp.float32)))
    smoothed = (
        along_depth(planar, slab_depth)
        .reshape(frames_here, slab_depth * extent)
        .astype(jnp.bfloat16)
    )
    picked = pick_columns(smoothed, positions)
    regrouped = lax.all_to_all(picked, "grp", split_axis=1, concat_axis=0, tiled=True)
    frame_count = regrouped.shape[0]
    subject_frames = frame_count // 2
    halves = regrouped.astype(jnp.float32).reshape(2, subject_frames, per_device)
    centered = (halves - jnp.mean(halves, axis=1, keepdims=True)).astype(jnp.bfloat16)
    order_rows = K + frame_count
    stacked = jnp.concatenate([subspace, centered.reshape(frame_count, per_device)], 0)
    widened = centered.astype(jnp.float32)
    power = lax.psum(jnp.sum(widened * widened, axis=(1, 2)), ("slab", "grp"))
    rows_here = order_rows // group_count
    first_row = lax.axis_index("grp") * rows_here
    gram_raw = lax.psum(
        jnp.dot(stacked, stacked.T, preferred_element_type=jnp.float32), ("slab", "grp")
    )
    owned = lax.dynamic_slice_in_dim(gram_raw, first_row, rows_here, 0)
    scales = lax.rsqrt(power / (masked * subject_frames) + epsilon)
    row_scale = jnp.concatenate([jnp.ones((K,), jnp.float32), jnp.repeat(scales, subject_frames)])
    owned_scale = lax.dynamic_slice_in_dim(row_scale, first_row, rows_here, 0)
    gram_rows = owned * (owned_scale[:, None] * row_scale[None, :]) / masked
    contract = (((0,), (0,)), ((), ()))
    from_basis = lax.dot_general(
        rotation[:K], subspace, contract, preferred_element_type=jnp.float32
    )
    from_first = lax.dot_general(
        rotation[K : K + subject_frames], centered[0], contract, preferred_element_type=jnp.float32
    )
    from_second = lax.dot_general(
        rotation[K + subject_frames :], centered[1], contract, preferred_element_type=jnp.float32
    )
    new_subspace = (from_basis + scales[0] * from_first + scales[1] * from_second).astype(
        jnp.bfloat16
    )
    return (gram_rows, new_subspace)


def solution(mesh):
    placed = (P("grp", "slab", None), P(("slab", "grp")), P(None, ("slab", "grp")), P())
    return jax.shard_map(
        body,
        mesh=mesh,
        in_specs=placed,
        out_specs=(P("grp", None), P(None, ("slab", "grp"))),
        check_vma=False,
    )
```

profile of v0, /device:TPU:0, one launch (start us, length us, event | category | flops | bytes accessed | tf_op | source)
XLA Modules:
  0.0 511.2 jit_solution(89150723595462847)
XLA Ops:
  7.2 0.0 all-reduce.5.cloned.1.call-start
  7.2 4.5 fusion.61
  11.7 2.5 collective-permute-start
  14.2 1.3 collective-permute-start.1
  15.5 0.7 reshape.63
  16.2 31.9 %all-gather = s32[8,1,1792]{2,1,0:T(1,128)S(1)} all-gather(s32[1,1,1792]{2,1,0:T(1,128)S(1)} %reshape.63), channel_id=1, replica_groups=mesh['slab'=4,'grp'=8] {'grp'}, dimensions={0}, use_global_device_ids=true | all-gather | bytes 64512 | tf_op jit(solution)/shard_map/all_gather | solution.py:99
  48.1 0.1 and_reduce_fusion
  48.2 0.1 broadcast_in_dim.55
  48.3 0.1 copy.22
  48.4 0.1 reduce.5
  48.8 0.1 broadcast_bitcast_fusion
  48.8 0.0 collective-permute-done
  48.9 0.0 collective-permute-done.1
  48.9 12.9 %maximum_convert_fusion = f32[32,18,10752]{2,0,1:T(8,128)} fusion(bf16[32,3,10752]{2,0,1:T(8,128)(2,1)} %collective-permute-done.1, bf16[32,12,10752]{2,0,1:T(8,128)(2,1)} %param.4, bf16[32,3,10752]{2,0,1:T(8,128)(2,1)S(1)} %collective-permute-done), kind=kLoop, calls=%fused_computation.29 | loop fusion | flops 18579456 | bytes 37158912 | tf_op jit(solution)/shard_map/convert_element_type | solution.py:103
  61.8 64.2 %multiply_add_fusion.1 = f32[32,18,10752]{2,0,1:T(8,128)} fusion(f32[32,18,10752]{2,0,1:T(8,128)} %maximum_convert_fusion, pred[10752]{0:T(1024)(128)(4,1)S(1)} %get-tuple-element.8, pred[10752]{0:T(1024)(128)(4,1)S(1)} %get-tuple-element.9, pred[10752]{0:T(1024)(128)(4,1)S(1)} %get-tuple-element.10, pred[10752]{0:T(1024)(128)(4,1)S(1)} %fusion.58, ...), kind=kLoop, calls=%fused_computation.7 | loop fusion | flops 123863040 | bytes 49620480 | tf_op jit(solution)/shard_map/add | solution.py:55
  125.9 64.0 %multiply_add_fusion = f32[32,18,10752]{2,0,1:T(8,128)} fusion(f32[32,18,10752]{2,0,1:T(8,128)} %multiply_add_fusion.1), kind=kLoop, calls=%fused_computation.1 | loop fusion | flops 80510976 | bytes 49545216 | tf_op jit(solution)/shard_map/add | solution.py:68
  189.9 40.4 %fusion.9 = bf16[32,12,10752]{2,0,1:T(8,128)(2,1)} fusion(f32[32,18,10752]{2,0,1:T(8,128)} %multiply_add_fusion), kind=kLoop, calls=%fused_computation.17 | loop fusion | flops 57802752 | bytes 123863040 | tf_op jit(solution)/shard_map/convert_element_type | solution.py:107
  230.3 12.2 %copy.23 = bf16[32,12,10752]{2,1,0:T(8,128)(2,1)} copy(bf16[32,12,10752]{2,0,1:T(8,128)(2,1)} %fusion.9) | data formatting | bytes 16515072 | tf_op jit(solution)/shard_map/convert_element_type | solution.py:107
  242.5 18.6 %convert_element_type.54 = bf16[32,1008,128]{2,1,0:T(8,128)(2,1)} reshape(bf16[32,12,10752]{2,1,0:T(8,128)(2,1)} %copy.23) | data formatting | bytes 16515072 | tf_op jit(solution)/shard_map/convert_element_type | solution.py:107
  261.0 8.6 %copy.24 = bf16[32,1008,128]{2,0,1:T(8,128)(2,1)} copy(bf16[32,1008,128]{2,1,0:T(8,128)(2,1)} %convert_element_type.54) | data formatting | bytes 16515072 | tf_op jit(solution)/shard_map/convert_element_type | solution.py:107
  269.7 4.1 gather_fusion
  273.8 0.4 copy.25
  274.1 1.0 gather.7
  275.1 0.1 broadcast_select_fusion
  275.2 0.2 copy.26
  275.4 24.6 %all_to_all.10 = bf16[32,8,1792]{2,0,1:T(8,128)(2,1)S(1)} all-to-all(bf16[32,8,1792]{2,0,1:T(8,128)(2,1)S(1)} %copy.26), channel_id=1, replica_groups=mesh['slab'=4,'grp'=8] {'grp'}, dimensions={1} | all-to-all | bytes 1835008 | tf_op jit(solution)/shard_map/all_to_all | solution.py:110
  300.1 0.2 bitcast_reduce_fusion
  300.4 0.2 fusion.24
  300.5 14.3 %fusion.19 = f32[1456,1456]{1,0:T(8,128)} fusion(bf16[256,1792]{1,0:T(8,128)(2,1)S(1)} %fusion.24, bf16[1200,1792]{1,0:T(8,128)(2,1)} %param.6), kind=kOutput, calls=%fused_computation.37 | convolution fusion | flops 7608287232 | bytes 13698048 | tf_op jit(solution)/shard_map/dot_general | solution.py:122
  314.9 0.0 all-reduce.5.cloned.1.call-update
  314.9 0.4 multiply_reduce_fusion
  315.3 0.1 reduce_sum.36
  315.4 0.1 reduce_sum.37
  315.5 40.8 %psum.15 = f32[2]{0:T(128)S(1)} all-reduce(f32[2]{0:T(128)S(1)} %reduce_sum.37), channel_id=1, replica_groups=mesh['slab'=4,'grp'=8] {'slab','grp'}, use_global_device_ids=true, to_apply=%region_5.6 | all-reduce | flops 2 | bytes 16 | tf_op jit(solution)/shard_map/psum | solution.py:118
  356.3 0.1 broadcast_bitcast_fusion.1
  356.4 0.1 concatenate.11
  356.5 0.1 convert_element_type.69
  356.6 0.1 pad_dynamic-slice_fusion
  356.7 0.6 fusion.62
  357.3 0.1 subtract_convert_fusion
  357.4 0.0 copy-start
  357.4 3.5 fusion.16
  360.9 3.1 fusion.17
  364.0 0.0 copy-done
  364.0 9.7 %fusion.18 = bf16[1200,1792]{1,0:T(8,128)(2,1)} fusion(f32[1200,1792]{1,0:T(8,128)S(1)} %fusion.17, f32[1200,1792]{1,0:T(8,128)S(1)} %fusion.16, bf16[1200,1792]{1,0:T(8,128)(2,1)} %param.6, bf16[1456,1200]{0,1:T(8,128)(2,1)S(1)} %copy-done), kind=kOutput, calls=%fused_computation.36 | convolution fusion | flops 5167411200 | bytes 28876800 | tf_op jit(solution)/shard_map/dot_general | solution.py:130
  373.7 128.2 %all-reduce.5.cloned.1.call-done = f32[1456,1456]{1,0:T(8,128)} async-done(((f32[1456,1456]{1,0:T(8,128)}), f32[1456,1456]{1,0:T(8,128)}) %all-reduce.5.cloned.1.call-update) | async-done | bytes 8479760 | tf_op jit(solution)/shard_map/psum | solution.py:121
  501.9 2.5 multiply_multiply_fusion
  (12 shorter events, 0.3 us)
Async XLA Ops:
  7.2 494.8 %all-reduce.5.cloned.1.call-start = ((), (), s32[]{:S(2)}) async-start(), calls=%async_computation.1 | async-start | bytes 17891328 | tf_op jit(solution)/shard_map/psum | solution.py:121
  11.7 37.2 %collective-permute-start = (bf16[32,3,10752]{2,0,1:T(8,128)(2,1)}, bf16[32,3,10752]{2,0,1:T(8,128)(2,1)S(1)}, u32[]{:S(2)}, u32[]{:S(2)}) collective-permute-start(bf16[32,3,10752]{2,0,1:T(8,128)(2,1)} %get-tuple-element.4), channel_id=1, source_target_pairs={{0,8},{8,16},{16,24},{1,9},{9,17},{17,25},{2,10},{10,18},{18,26},{... | collective-permute-start | bytes 6193160 | tf_op jit(solution)/shard_map/ppermute | solution.py:26
  14.2 34.6 %collective-permute-start.1 = (bf16[32,3,10752]{2,0,1:T(8,128)(2,1)}, bf16[32,3,10752]{2,0,1:T(8,128)(2,1)}, u32[]{:S(2)}, u32[]{:S(2)}) collective-permute-start(bf16[32,3,10752]{2,0,1:T(8,128)(2,1)} %get-tuple-element.5), channel_id=1, source_target_pairs={{8,0},{16,8},{24,16},{9,1},{17,9},{25,17},{10,2},{18,10},{26,18},{... | collective-permute-start | bytes 6193160 | tf_op jit(solution)/shard_map/ppermute | solution.py:28
  357.4 6.6 %copy-start = (bf16[1456,1200]{0,1:T(8,128)(2,1)S(1)}, bf16[1456,1200]{0,1:T(8,128)(2,1)}, u32[]{:S(2)}) copy-start(bf16[1456,1200]{0,1:T(8,128)(2,1)} %param.7) | copy-start | bytes 10483204
Sparse Core Ops, SparseCore 0:
  315.0 186.8 all-reduce.4
where the time goes:
time: 512 us; the launch traced here: 511 us
  other arithmetic  186 us (36%)
  waiting for transfers between devices  128 us (25%)
  blocking collectives  97.3 us (19%)
  local copies, waits for them, and re-layouts  51.4 us (10%)
  matrix products  30.6 us (6%)
  between operations  14.2 us (3%)
    psum x1, waiting for transfers between devices, body(): lax.psum(jnp.dot(stacked, stacked.T, preferred_element_type=jnp.float32),...  128 us
    add x1, other arithmetic, along_rows(): summed = summed + weights[offset + RAD] * jnp.where(inside, shifted, 0.0)  64.2 us
    add x1, other arithmetic, along_columns(): summed = summed + weights[offset + RAD] * shifted  64 us
    psum x1, blocking collectives, body(): power = lax.psum(jnp.sum(widened * widened, axis=(1, 2)), ('slab', 'grp'))  40.8 us
    convert_element_type x1, other arithmetic, body(): smoothed = along_depth(planar, slab_depth).reshape(frames_here, slab_dept...  40.4 us
    convert_element_type x3, local copies, waits for them, and re-layouts, body(): smoothed = along_depth(planar, slab_depth).reshape(frames_here, slab_dept...  39.4 us
    all_gather x1, blocking collectives, body(): lax.all_gather(mask_index, 'grp', axis=0, tiled=True)  31.9 us
    all_to_all x1, blocking collectives, body(): lax.all_to_all(picked, 'grp', split_axis=1, concat_axis=0, tiled=True)  24.6 us
  transfers between devices with their start and end apart: 3, of which 1 were waited for; matrix products, arithmetic and copies ran while one was open for 4% of the time, Pallas kernels for 0%

commit v1 on v0

v1 whole, which is shorter than its diff:
```python
import functools
import math

import jax
import jax.numpy as jnp
import numpy as np
from jax import lax
from jax.experimental import pallas as pl
from jax.experimental.pallas import tpu as pltpu
from jax.sharding import PartitionSpec as P

NX = 96
RUN = 128
RAD = 3
K = 1200
MESH = pl.DeviceIdType.MESH

smooth_sigma = 1.0617
epsilon = 1e-06

WIDE = 2 * RUN
LEFT = 3 * RUN
SPAN = 8 * RUN


def tap_weights():
    unscaled = [
        math.exp(-offset * offset / (2.0 * smooth_sigma * smooth_sigma))
        for offset in range(-RAD, RAD + 1)
    ]
    summed = sum(unscaled)
    return [weight / summed for weight in unscaled]


def plane_weights():
    taps = np.array(tap_weights())
    kinds = NX // math.gcd(WIDE, NX)
    out = np.zeros((kinds, SPAN, WIDE))
    for kind in range(kinds):
        target = np.arange(WIDE)
        column = (kind * WIDE + target) % NX
        for dy in range(-RAD, RAD + 1):
            for dx in range(-RAD, RAD + 1):
                inside = (column + dx >= 0) & (column + dx < NX)
                source = target + LEFT + dy * NX + dx
                out[kind, source[inside], target[inside]] = taps[dy + RAD] * taps[dx + RAD]
    return out.astype(jnp.bfloat16)


def exchange_kernel(total, groups, summed, x_ref, out_ref, landed, send_sem, recv_sem):
    me = lax.axis_index("slab") * groups + lax.axis_index("grp")
    barrier = pltpu.get_barrier_semaphore()

    def place(peer):
        return (peer // groups, lax.rem(peer, groups))

    def greet(step, _):
        pl.semaphore_signal(
            barrier, inc=1, device_id=place(lax.rem(me + step, total)), device_id_type=MESH
        )
        return 0

    lax.fori_loop(1, total, greet, 0)
    pl.semaphore_wait(barrier, total - 1)

    def copy(step):
        return pltpu.make_async_remote_copy(
            src_ref=x_ref,
            dst_ref=landed.at[step],
            send_sem=send_sem.at[step],
            recv_sem=recv_sem.at[step],
            device_id=place(lax.rem(me + step, total)),
            device_id_type=MESH,
        )

    def start(step, _):
        copy(step).start()
        return 0

    def finish(step, _):
        copy(step).wait()
        return 0

    lax.fori_loop(1, total, start, 0)
    landed[0] = x_ref[...]
    lax.fori_loop(1, total, finish, 0)
    if summed:
        out_ref[...] = jnp.sum(landed[...], axis=0)
    else:
        def put(step, _):
            out_ref[lax.rem(me + total - step, total)] = landed[step]
            return 0

        lax.fori_loop(0, total, put, 0)


def exchange(x, summed, collective_id):
    groups = lax.axis_size("grp")
    total = groups * lax.axis_size("slab")
    shape = x.shape if summed else (total,) + x.shape
    return pl.pallas_call(
        functools.partial(exchange_kernel, total, groups, summed),
        out_shape=jax.ShapeDtypeStruct(shape, x.dtype),
        in_specs=[pl.BlockSpec(memory_space=pltpu.VMEM)],
        out_specs=pl.BlockSpec(memory_space=pltpu.VMEM),
        scratch_shapes=[
            pltpu.VMEM((total,) + x.shape, x.dtype),
            pltpu.SemaphoreType.DMA((total,)),
            pltpu.SemaphoreType.DMA((total,)),
        ],
        compiler_params=pltpu.CompilerParams(
            collective_id=collective_id, has_side_effects=True
        ),
    )(x)


def smooth_kernel(depth, frames, own, up, z_ref, r_ref, x_ref, w_ref, own_ref, up_ref, down_ref, y_ref):
    taps = tap_weights()
    kinds = w_ref.shape[0]
    steps = y_ref.shape[0] // (2 * kinds)

    def planar(step, _):
        for kind in range(kinds):
            place = step * kinds + kind
            begin = pl.multiple_of(place * WIDE, WIDE)
            found = jnp.dot(
                x_ref[:, pl.ds(begin, SPAN)], w_ref[kind], preferred_element_type=jnp.float32
            )
            y_ref[2 * place] = found[:, :RUN]
            y_ref[2 * place + 1] = found[:, RUN:]
        return 0

    lax.fori_loop(0, steps, planar, 0)

    def picked(run):
        z = z_ref[run]
        r = r_ref[run]
        total = None
        for offset in range(-RAD, RAD + 1):
            at = z + offset
            weight = jnp.where((at >= 0) & (at < depth), jnp.float32(taps[offset + RAD]), 0.0)
            row = pl.multiple_of(jnp.clip(at, 0, depth - 1) * frames, frames)
            term = weight * y_ref[r, pl.ds(row, frames), :]
            total = term if total is None else total + term
        return total

    def put(ref, first):
        def one(run, _):
            ref[run] = picked(run + first).astype(ref.dtype)
            return 0

        lax.fori_loop(0, ref.shape[0], one, 0)

    put(up_ref, own)
    put(down_ref, own + up)
    put(own_ref, 0)


def smooth(cells, weights, planes_at, runs_at, depth, frames, extent, own, rim):
    vmem = pl.BlockSpec(memory_space=pltpu.VMEM)
    smem = pl.BlockSpec(memory_space=pltpu.SMEM)
    return pl.pallas_call(
        functools.partial(smooth_kernel, depth, frames, own, rim),
        out_shape=(
            jax.ShapeDtypeStruct((own, frames, RUN), jnp.float32),
            jax.ShapeDtypeStruct((rim, frames, RUN), jnp.bfloat16),
            jax.ShapeDtypeStruct((rim, frames, RUN), jnp.bfloat16),
        ),
        in_specs=[smem, smem, vmem, vmem],
        out_specs=(vmem, vmem, vmem),
        scratch_shapes=[pltpu.VMEM((extent // RUN, depth * frames, RUN), jnp.float32)],
        compiler_params=pltpu.CompilerParams(vmem_limit_bytes=48 * 1024 * 1024),
    )(planes_at, runs_at, cells, weights)


def body(raw_frames, mask_index, subspace, rotation):
    frames_here, slab_depth, extent = raw_frames.shape
    per_device = subspace.shape[1]
    group_count = lax.axis_size("grp")
    slab_count = lax.axis_size("slab")
    masked = per_device * slab_count * group_count
    frame_count = frames_here * group_count
    subject_frames = frame_count // 2
    order_rows = K + frame_count
    rows_here = order_rows // group_count
    first_row = lax.axis_index("grp") * rows_here
    slab = lax.axis_index("slab")
    runs_here = per_device // RUN
    own = runs_here * group_count
    rim = own * RAD // slab_depth
    both = ("slab", "grp")

    basis_part = lax.dot_general(
        subspace, subspace, (((1,), (1,)), ((), ())), preferred_element_type=jnp.float32
    ).astype(jnp.bfloat16)
    basis_rows = lax.psum_scatter(
        jnp.pad(basis_part, ((0, frame_count), (0, 0))), "grp", scatter_dimension=0, tiled=True
    )
    basis_rows = lax.psum(basis_rows.astype(jnp.float32), "slab")

    starts = exchange(mask_index.reshape(runs_here, RUN), False, 1)[:, :, 0]
    starts = starts.reshape(slab_count, own) - slab * (slab_depth * extent)
    wanted = jnp.concatenate(
        [
            lax.dynamic_index_in_dim(starts, slab, 0, False),
            lax.dynamic_index_in_dim(starts, jnp.minimum(slab + 1, slab_count - 1), 0, False)[:rim],
            lax.dynamic_index_in_dim(starts, jnp.maximum(slab - 1, 0), 0, False)[own - rim :],
        ]
    )
    planes_at = jnp.floor_divide(wanted, extent)
    runs_at = (wanted - planes_at * extent) // RUN

    cells = jnp.pad(
        raw_frames.transpose(1, 0, 2), ((0, 0), (0, 0), (LEFT, SPAN - WIDE - LEFT))
    ).reshape(slab_depth * frames_here, -1)
    inner, upward, downward = smooth(
        cells, jnp.asarray(plane_weights()), planes_at, runs_at,
        slab_depth, frames_here, extent, own, rim,
    )
    ends = slab_count - 1
    from_below = lax.ppermute(upward, "slab", [(i, i + 1) for i in range(ends)])
    from_above = lax.ppermute(downward, "slab", [(i + 1, i) for i in range(ends)])
    smoothed = jnp.concatenate(
        [
            inner[:rim] + from_below.astype(jnp.float32),
            inner[rim : own - rim],
            inner[own - rim :] + from_above.astype(jnp.float32),
        ]
    ).astype(jnp.bfloat16)
    regrouped = lax.all_to_all(smoothed, "grp", split_axis=0, concat_axis=0, tiled=True)
    halves = (
        regrouped.reshape(group_count, runs_here, frames_here, RUN)
        .transpose(0, 2, 1, 3)
        .reshape(2, subject_frames, per_device)
        .astype(jnp.float32)
    )
    centered = (halves - jnp.mean(halves, axis=1, keepdims=True)).astype(jnp.bfloat16)
    widened = centered.astype(jnp.float32)
    squares = jnp.sum(widened * widened, axis=(1, 2))
    power = exchange(jnp.broadcast_to(jnp.pad(squares, (0, 6))[:, None], (8, RUN)), True, 2)[:2, 0]
    centered = centered.reshape(frame_count, per_device)
    stacked = jnp.concatenate([subspace, centered], 0)
    data_part = lax.psum(
        lax.dot_general(
            stacked, centered, (((1,), (1,)), ((), ())), preferred_element_type=jnp.float32
        ),
        both,
    )
    scales = lax.rsqrt(power / (masked * subject_frames) + epsilon)
    row_scale = jnp.concatenate([jnp.ones((K,), jnp.float32), jnp.repeat(scales, subject_frames)])

    turned = (rotation.astype(jnp.float32) * row_scale[:, None]).astype(jnp.bfloat16)
    new_subspace = lax.dot_general(
        turned, stacked, (((0,), (0,)), ((), ())), preferred_element_type=jnp.float32
    ).astype(jnp.bfloat16)

    right = lax.dynamic_slice_in_dim(data_part, first_row, rows_here, 0)
    low = jnp.pad(data_part[:K].T, ((rows_here, rows_here), (0, 0)))
    low = lax.dynamic_slice_in_dim(low, jnp.maximum(first_row - K + rows_here, 0), rows_here, 0)
    owned = jnp.concatenate([basis_rows + low, right], 1)
    owned_scale = lax.dynamic_slice_in_dim(row_scale, first_row, rows_here, 0)
    gram_rows = owned * (owned_scale[:, None] * row_scale[None, :]) / masked
    return (gram_rows, new_subspace)


def solution(mesh):
    placed = (P("grp", "slab", None), P(("slab", "grp")), P(None, ("slab", "grp")), P())
    return jax.shard_map(
        body,
        mesh=mesh,
        in_specs=placed,
        out_specs=(P("grp", None), P(None, ("slab", "grp"))),
        check_vma=False,
    )
```

time: 512 us -> 425 us (0.83)
  other arithmetic: 186 us -> 11.9 us
  waiting for transfers between devices: 128 us -> 277 us
  blocking collectives: 97.3 us -> 27.8 us
  Pallas kernels: 0 us -> 47.9 us
  local copies, waits for them, and re-layouts: 51.4 us -> 16.4 us
    unnamed x1 -> x4, waiting for transfers between devices: 0.02 us -> 145 us
    add x2 -> x1, other arithmetic: 128 us -> 1.7 us  [body(): owned = jnp.concatenate([basis_rows + low, right], 1)]
    convert_element_type x3 -> x2, other arithmetic: 53.4 us -> 2.71 us  [the longest x1 2.47 us: body(): basis_rows = lax.psum(basis_rows.astype(jnp.float32), 'slab')]
    pallas_call x0 -> x3, Pallas kernels: none -> 47.9 us  [the longest x2 27.7 us: exchange(): pl.pallas_call(functools.partial(exchange_kernel, total, groups, summed),...]
    psum x1 -> x0, blocking collectives: 40.8 us -> none  [body(): power = lax.psum(jnp.sum(widened * widened, axis=(1, 2)), ('slab', 'grp'))]
    convert_element_type x3 -> x1, local copies, waits for them, and re-layouts: 39.4 us -> 1.63 us  [body(): halves = regrouped.reshape(group_count, runs_here, frames_here, RUN).tran...]
    all_gather x1 -> x0, blocking collectives: 31.9 us -> none  [body(): lax.all_gather(mask_index, 'grp', axis=0, tiled=True)]
    pad x0 -> x3, local copies, waits for them, and re-layouts: none -> 9.83 us  [the longest x1 7.65 us: body(): jnp.pad(raw_frames.transpose(1, 0, 2), ((0, 0), (0, 0), (LEFT, SPAN - WID...]
  transfers between devices with their start and end apart: 3 -> 5, of which waited for: 1 -> 4; matrix products, arithmetic and copies ran while one was open for 4% -> 7% of each run, Pallas kernels for 0% -> 3%
where the time goes in v1:
time: 425 us
  waiting for transfers between devices  277 us (65%)
  Pallas kernels  47.9 us (11%)
  blocking collectives  27.8 us (7%)
  matrix products  25.5 us (6%)
  local copies, waits for them, and re-layouts  16.4 us (4%)
  between operations  14.6 us (3%)
  other arithmetic  11.9 us (3%)
    unnamed x4, waiting for transfers between devices  145 us
    psum x1, waiting for transfers between devices, body(): lax.psum(lax.dot_general(stacked, centered, (((1,), (1,)), ((), ())), pre...  92.3 us
    psum x1, waiting for transfers between devices, body(): basis_rows = lax.psum(basis_rows.astype(jnp.float32), 'slab')  37.2 us
    all_to_all x1, blocking collectives, body(): lax.all_to_all(smoothed, 'grp', split_axis=0, concat_axis=0, tiled=True)  27.8 us
    pallas_call x2, Pallas kernels, exchange(): pl.pallas_call(functools.partial(exchange_kernel, total, groups, summed),...  27.7 us
    pallas_call x1, Pallas kernels, smooth(): pl.pallas_call(functools.partial(smooth_kernel, depth, frames, own, rim),...  20.2 us
    dot_general x1, matrix products, body(): lax.dot_general(turned, stacked, (((0,), (0,)), ((), ())), preferred_elem...  11.2 us
    dot_general x1, matrix products, body(): lax.dot_general(subspace, subspace, (((1,), (1,)), ((), ())), preferred_e...  9.41 us
  transfers between devices with their start and end apart: 5, of which 4 were waited for; matrix products, arithmetic and copies ran while one was open for 7% of the time, Pallas kernels for 3%

profile of v1, /device:TPU:0, one launch (start us, length us, event | category | flops | bytes accessed | tf_op | source)
XLA Modules:
  0.0 424.6 jit_solution(1354649974264972486)
XLA Ops:
  7.2 0.0 all-reduce.12.cloned.1.call-start
  7.2 15.4 %shard_map.68 = s32[32,14,128]{2,1,0:T(8,128)} custom-call(s32[14,128]{1,0:T(8,128)} %bitcast.41), custom_call_target="tpu_custom_call" | custom-call | tf_op jit(solution)/shard_map/pallas_call | solution.py:101
  22.7 1.6 subtract_reduce_fusion
  24.2 0.1 sub.48
  24.3 0.1 slice_bitcast_fusion.1
  24.4 7.6 %pad.18 = bf16[12,32,11520]{2,1,0:T(8,128)(2,1)} pad(bf16[12,32,10752]{2,1,0:T(8,128)(2,1)} %bitcast.38, bf16[]{:T(256)} %constant.57.clone.1), padding=0_0x0_0x384_384 | pad | bytes 17104898 | tf_op jit(solution)/shard_map/jit(_pad)/pad | solution.py:213
  32.0 0.1 and_select_fusion
  32.1 20.2 %shard_map.69 = (f32[112,32,128]{2,1,0:T(8,128)S(1)}, bf16[28,32,128]{2,1,0:T(8,128)(2,1)S(1)}, bf16[28,32,128]{2,1,0:T(8,128)(2,1)S(1)}) custom-call(s32[168]{0:T(256)S(1)} %get-tuple-element.15.z_ref, s32[168]{0:T(256)S(1)} %get-tuple-element.14.r_ref, bf16[384,11520]{1,0:T(8,128)(2,1)} %bitcast.36, bf16[3,1024,256]{2,1,0:T(8,128)(2,1)S(1)} %copy-done), custom_call_target="tpu_custom_call" | custom-call | tf_op jit(solution)/shard_map/pallas_call | solution.py:162
  52.3 1.6 collective-permute-start
  53.9 1.3 collective-permute-start.1
  55.2 0.1 slice.51
  55.3 2.4 collective-permute-done.1
  57.8 0.2 add_convert_fusion.1
  57.9 0.1 pad_maximum_fusion.3
  58.0 27.8 %all_to_all.5 = bf16[112,32,128]{2,1,0:T(8,128)(2,1)S(1)} all-to-all(bf16[112,32,128]{2,1,0:T(8,128)(2,1)S(1)} %pad_maximum_fusion.3), channel_id=1, replica_groups=mesh['slab'=4,'grp'=8] {'grp'}, dimensions={0} | all-to-all | bytes 1835008 | tf_op jit(solution)/shard_map/all_to_all | solution.py:230
  85.9 1.6 copy.15
  87.5 0.2 convert.18
  87.8 1.0 bitcast_reduce_fusion
  88.9 2.1 fusion.3
  91.0 5.0 %fusion = f32[1456,256]{1,0:T(8,128)} fusion(bf16[256,1792]{1,0:T(8,128)(2,1)S(1)} %fusion.3, bf16[1200,1792]{1,0:T(8,128)(2,1)} %param.7), kind=kOutput, calls=%fused_computation.4 | convolution fusion | flops 1346322432 | bytes 6709248 | tf_op jit(solution)/shard_map/dot_general | solution.py:244
  96.0 0.0 all-reduce.12.cloned.1.call-update
  96.0 0.0 all-reduce.14.cloned.1.call-start
  96.1 9.4 %convolution_convert_fusion.1 = bf16[1200,1200]{0,1:T(8,128)(2,1)S(1)} fusion(bf16[1200,1792]{1,0:T(8,128)(2,1)} %param.7), kind=kOutput, calls=%fused_computation.1 | convolution fusion | flops 5162399744 | bytes 7180800 | tf_op jit(solution)/shard_map/dot_general | solution.py:193
  105.5 2.2 pad.17
  107.7 0.0 all-reduce.14.cloned.1.call-update
  107.7 0.2 all-reduce.10.cloned.1.call-start
  107.9 0.4 copy-done.2
  108.3 0.6 dynamic-slice
  109.6 1.1 multiply_reduce_fusion
  110.7 0.1 reduce_sum.36
  110.8 0.1 reduce_sum.37
  111.0 0.7 broadcast_in_dim.4.x_ref
  111.6 12.3 %shard_map.70 = f32[8,128]{1,0:T(8,128)} custom-call(f32[8,128]{1,0:T(8,128)} %broadcast_in_dim.4.x_ref), custom_call_target="tpu_custom_call" | custom-call | tf_op jit(solution)/shard_map/pallas_call | solution.py:101
  123.9 0.8 rsqrt_reduce_fusion
  124.7 0.1 broadcast_bitcast_fusion
  124.8 0.1 concatenate.20
  124.9 0.1 pad_dynamic-slice_fusion.1
  125.0 11.2 %convolution_convert_fusion = bf16[1200,1792]{1,0:T(8,128)(2,1)} fusion(bf16[256,1792]{1,0:T(8,128)(2,1)S(1)} %fusion.3, bf16[1200,1792]{1,0:T(8,128)(2,1)} %param.7, bf16[1456,1200]{0,1:T(8,128)(2,1)} %param.8, f32[1456]{0:T(1024)S(1)} %concatenate.20), kind=kOutput, calls=%fused_computation | convolution fusion | flops 6279793664 | bytes 13019328 | tf_op jit(solution)/shard_map/dot_general | solution.py:253
  136.1 92.3 %all-reduce.12.cloned.1.call-done = f32[1456,256]{1,0:T(8,128)} async-done(((f32[1456,256]{1,0:T(8,128)}), f32[1456,256]{1,0:T(8,128)}) %all-reduce.12.cloned.1.call-update) | async-done | bytes 1490960 | tf_op jit(solution)/shard_map/psum | solution.py:243
  228.5 1.1 constant_dynamic-slice_fusion
  229.6 0.1 copy.16
  229.7 145.2 %all-reduce.14.cloned.1.call-done = bf16[1456,1200]{0,1:T(8,128)(2,1)} async-done(((bf16[1456,1200]{0,1:T(8,128)(2,1)}), bf16[1456,1200]{0,1:T(8,128)(2,1)}) %all-reduce.14.cloned.1.call-update) | async-done | bytes 3494416
  374.9 2.5 dynamic-slice_convert_fusion
  377.4 0.1 slice_bitcast_fusion
  377.5 37.2 %all-reduce.10.cloned.1.call-done = f32[182,1200]{0,1:T(8,128)} async-done(((f32[182,1200]{0,1:T(8,128)}), f32[182,1200]{0,1:T(8,128)}) %all-reduce.10.cloned.1.call-update) | async-done | bytes 873616 | tf_op jit(solution)/shard_map/psum | solution.py:199
  414.7 1.7 fusion.5
  416.4 0.3 fusion.4
  416.7 1.4 copy.17
  (14 shorter events, 0.2 us)
Async XLA Ops:
  7.2 221.3 %all-reduce.12.cloned.1.call-start = ((), (), s32[]{:S(2)}) async-start(), calls=%async_computation.2 | async-start | bytes 2981888 | tf_op jit(solution)/shard_map/psum | solution.py:243
  24.4 7.7 %copy-start = (bf16[3,1024,256]{2,1,0:T(8,128)(2,1)S(1)}, bf16[3,1024,256]{2,1,0:T(8,128)(2,1)}, u32[]{:S(2)}) copy-start(bf16[3,1024,256]{2,1,0:T(8,128)(2,1)} %constant.78.clone.w_ref) | copy-start | bytes 4718596
  52.3 3.0 collective-permute-start
  53.9 3.8 collective-permute-start.1
  96.0 278.9 %all-reduce.14.cloned.1.call-start = ((), (), s32[]{:S(2)}) async-start(), calls=%async_computation.3 | async-start | bytes 7372800
  107.7 0.7 copy-start.2
  107.7 307.0 %all-reduce.10.cloned.1.call-start = ((), (), s32[]{:S(2)}) async-start(), calls=%async_computation.1 | async-start | bytes 2457600 | tf_op jit(solution)/shard_map/psum | solution.py:199
  228.5 148.9 %copy-start.1 = (f32[1456,256]{1,0:T(8,128)S(1)}, f32[1456,256]{1,0:T(8,128)}, u32[]{:S(2)}) copy-start(f32[1456,256]{1,0:T(8,128)} %all-reduce.12.cloned.1.call-done) | copy-start | bytes 4472836
Sparse Core Ops, SparseCore 0:
  96.1 132.3 all-reduce.11
  232.1 142.7 all-reduce.13
  377.5 37.0 all-reduce.9

commit v2 on v1

--- a/solution.py
+++ b/solution.py
@@ -114,10 +114,162 @@
     )(x)
 
 
-def smooth_kernel(depth, frames, own, up, z_ref, r_ref, x_ref, w_ref, own_ref, up_ref, down_ref, y_ref):
-    taps = tap_weights()
+def axes_of(groups, slabs):
+    outer = 4 if groups % 4 == 0 else 1
+    cores = 2 if slabs % 2 == 0 else 1
+    return outer, groups // outer, slabs // cores, cores
+
+
+def coordinates(sizes):
+    slab, grp = lax.axis_index("slab"), lax.axis_index("grp")
+    return [grp // sizes[1], lax.rem(grp, sizes[1]), slab // sizes[3], lax.rem(slab, sizes[3])]
+
+
+def device_at(at, sizes):
+    return (at[2] * sizes[3] + at[3], at[0] * sizes[1] + at[1])
+
+
+def moved(at, sizes, axis, step):
+    other = lax.rem(at[axis] + step, sizes[axis])
+    return at[:axis] + [other] + at[axis + 1 :], other
+
+
+def greet_all(sizes):
+    barrier = pltpu.get_barrier_semaphore()
+    at = coordinates(sizes)
+    count = 0
+    for axis, size in enumerate(sizes):
+        for step in range(1, size):
+            there, _ = moved(at, sizes, axis, step)
+            pl.semaphore_signal(
+                barrier, inc=1, device_id=device_at(there, sizes), device_id_type=MESH
+            )
+            count += 1
+    return barrier, count
+
+
+class Scatter:
+    def __init__(self, sizes, axis, src, landed, out, sems):
+        self.sizes, self.axis, self.src, self.landed, self.out = sizes, axis, src, landed, out
+        self.send_sem, self.recv_sem = sems
+        self.at = coordinates(sizes)
+
+    def part(self, where):
+        return self.src.at[(slice(None),) * self.axis + (where,)]
+
+    def copy(self, step):
+        there, other = moved(self.at, self.sizes, self.axis, step)
+        return pltpu.make_async_remote_copy(
+            src_ref=self.part(other),
+            dst_ref=self.landed.at[step - 1],
+            send_sem=self.send_sem.at[self.axis, step],
+            recv_sem=self.recv_sem.at[self.axis, step],
+            device_id=device_at(there, self.sizes),
+            device_id_type=MESH,
+        )
+
+    def start(self):
+        for step in range(1, self.sizes[self.axis]):
+            self.copy(step).start()
+
+    def finish(self):
+        for step in range(1, self.sizes[self.axis]):
+            self.copy(step).wait()
+        mine = self.part(self.at[self.axis])
+        lead = self.sizes[: self.axis]
+        total = math.prod(lead)
+
+        def add(index, _):
+            where = []
+            for size in reversed(lead):
+                where.insert(0, lax.rem(index, size))
+                index = index // size
+            where = tuple(where)
+            value = mine[where].astype(jnp.float32)
+            for step in range(self.sizes[self.axis] - 1):
+                value = value + self.landed[(step,) + where].astype(jnp.float32)
+            self.out[where] = value.astype(self.out.dtype)
+            return 0
+
+        lax.fori_loop(0, total, add, 0)
+
+
+class Gather:
+    def __init__(self, sizes, axis, full, first, sems):
+        self.sizes, self.axis, self.full, self.first = sizes, axis, full, first
+        self.send_sem, self.recv_sem = sems
+        self.at = coordinates(sizes)
+
+    def copy(self, step):
+        there, _ = moved(self.at, self.sizes, self.axis, step)
+        where = (slice(None),) * (self.axis - self.first) + tuple(self.at[self.axis :])
+        return pltpu.make_async_remote_copy(
+            src_ref=self.full.at[where],
+            dst_ref=self.full.at[where],
+            send_sem=self.send_sem.at[self.axis, step],
+            recv_sem=self.recv_sem.at[self.axis, step],
+            device_id=device_at(there, self.sizes),
+            device_id_type=MESH,
+        )
+
+    def start(self):
+        for step in range(1, self.sizes[self.axis]):
+            self.copy(step).start()
+
+    def finish(self):
+        for step in range(1, self.sizes[self.axis]):
+            self.copy(step).wait()
+
+
+def stage_scratch(sizes, piece):
+    out = []
+    for axis in range(3, -1, -1):
+        shape = tuple(sizes[:axis]) + piece
+        out.append(pltpu.VMEM((sizes[axis] - 1,) + shape, jnp.bfloat16))
+        if axis:
+            out.append(pltpu.VMEM(shape, jnp.bfloat16))
+    return out
+
+
+def stage_sems(sizes):
+    most = max(sizes)
+    return [pltpu.SemaphoreType.DMA((4, most)) for _ in range(4)]
+
+
+def scatter_stages(sizes, src, bufs, result, sems):
+    stages = []
+    for number, axis in enumerate(range(3, -1, -1)):
+        landed = bufs[2 * number]
+        out = bufs[2 * number + 1] if axis else result
+        stages.append(Scatter(sizes, axis, src, landed, out, sems))
+        src = out
+    return stages
+
+
+def smooth_kernel(sizes, depth, frames, own, rim, z_ref, r_ref, x_ref, w_ref, gram_ref,
+                  out_ref, rows_ref, y_ref, full, up_ref, down_ref, below, above, picked_ref,
+                  regrouped, halo_send, halo_recv, all_send, all_recv,
+                  s_send, s_recv, g_send, g_recv, *bufs):
     kinds = w_ref.shape[0]
-    steps = y_ref.shape[0] // (2 * kinds)
+    steps = y_ref.shape[0] // (2 * kinds * depth)
+    groups, slabs = sizes[0] * sizes[1], sizes[2] * sizes[3]
+    slab, grp = lax.axis_index("slab"), lax.axis_index("grp")
+    at = coordinates(sizes)
+    runs = own // groups
+    upper = lax.rem(slab + 1, slabs)
+    lower = lax.rem(slab + slabs - 1, slabs)
+
+    barrier, count = greet_all(sizes)
+    for other in (upper, lower):
+        pl.semaphore_signal(barrier, inc=1, device_id=(other, grp), device_id_type=MESH)
+    for step in range(1, groups):
+        pl.semaphore_signal(
+            barrier, inc=1, device_id=(slab, lax.rem(grp + step, groups)), device_id_type=MESH
+        )
+    pl.semaphore_wait(barrier, count + 2 + groups - 1)
+
+    scatter = scatter_stages(sizes, gram_ref, bufs, full.at[at[2], at[3]], (s_send, s_recv))
+    gather = [Gather(sizes, axis, full, 2, (g_send, g_recv)) for axis in (2, 3)]
 
     def planar(step, _):
         for kind in range(kinds):
@@ -126,21 +278,16 @@
             found = jnp.dot(
                 x_ref[:, pl.ds(begin, SPAN)], w_ref[kind], preferred_element_type=jnp.float32
             )
-            y_ref[2 * place] = found[:, :RUN]
-            y_ref[2 * place + 1] = found[:, RUN:]
+            for side in range(2):
+                y_ref[pl.ds((2 * place + side) * depth, depth)] = found[
+                    :, side * RUN : (side + 1) * RUN
+                ].reshape(depth, frames, RUN)
         return 0
 
-    lax.fori_loop(0, steps, planar, 0)
-
     def picked(run):
-        z = z_ref[run]
-        r = r_ref[run]
         total = None
-        for offset in range(-RAD, RAD + 1):
-            at = z + offset
-            weight = jnp.where((at >= 0) & (at < depth), jnp.float32(taps[offset + RAD]), 0.0)
-            row = pl.multiple_of(jnp.clip(at, 0, depth - 1) * frames, frames)
-            term = weight * y_ref[r, pl.ds(row, frames), :]
+        for tap in range(2 * RAD + 1):
+            term = z_ref[run * (2 * RAD + 1) + tap] * y_ref[r_ref[run * (2 * RAD + 1) + tap]]
             total = term if total is None else total + term
         return total
 
@@ -149,28 +296,146 @@
             ref[run] = picked(run + first).astype(ref.dtype)
             return 0
 
-        lax.fori_loop(0, ref.shape[0], one, 0)
+        lax.fori_loop(0, rim, one, 0)
+
+    def halo(src, dst, number, other):
+        return pltpu.make_async_remote_copy(
+            src_ref=src, dst_ref=dst, send_sem=halo_send.at[number], recv_sem=halo_recv.at[number],
+            device_id=(other, grp), device_id_type=MESH,
+        )
+
+    scatter[0].start()
+    early = steps // 3
+    lax.fori_loop(0, early, planar, 0)
+    scatter[0].finish()
+    scatter[1].start()
+    lax.fori_loop(early, steps, planar, 0)
 
     put(up_ref, own)
-    put(down_ref, own + up)
-    put(own_ref, 0)
-
-
-def smooth(cells, weights, planes_at, runs_at, depth, frames, extent, own, rim):
+    halo_up = halo(up_ref, below, 0, upper)
+    halo_up.start()
+    put(down_ref, own + rim)
+    halo_down = halo(down_ref, above, 1, lower)
+    halo_down.start()
+
+    def inner(run, _):
+        picked_ref[run] = picked(run).astype(picked_ref.dtype)
+        return 0
+
+    lax.fori_loop(rim, own - rim, inner, 0)
+    halo_up.wait()
+    halo_down.wait()
+    low_part = jnp.where(slab > 0, 1.0, 0.0)
+    high_part = jnp.where(slab < slabs - 1, 1.0, 0.0)
+
+    def edge(run, _):
+        picked_ref[run] = (picked(run) + low_part * below[run].astype(jnp.float32)).astype(
+            picked_ref.dtype
+        )
+        last = run + own - rim
+        picked_ref[last] = (picked(last) + high_part * above[run].astype(jnp.float32)).astype(
+            picked_ref.dtype
+        )
+        return 0
+
+    lax.fori_loop(0, rim, edge, 0)
+
+    def trade(step):
+        other = lax.rem(grp + step, groups)
+        return pltpu.make_async_remote_copy(
+            src_ref=picked_ref.at[pl.ds(other * runs, runs)], dst_ref=regrouped.at[grp],
+            send_sem=all_send.at[step], recv_sem=all_recv.at[step],
+            device_id=(slab, other), device_id_type=MESH,
+        )
+
+    for step in range(1, groups):
+        trade(step).start()
+    regrouped[grp] = picked_ref[pl.ds(grp * runs, runs)]
+
+    scatter[1].finish()
+    for stage in scatter[2:]:
+        stage.start()
+        stage.finish()
+    for stage in gather:
+        stage.start()
+        stage.finish()
+    for step in range(1, groups):
+        trade(step).wait()
+    rows_ref[...] = full[...]
+
+    half = groups // 2
+    for run in range(runs):
+        lanes = slice(run * RUN, (run + 1) * RUN)
+        for subject in range(2):
+            block = regrouped[subject * half : (subject + 1) * half, run].astype(jnp.float32)
+            block = block.reshape(half * frames, RUN)
+            mean = jnp.sum(block, axis=0, keepdims=True) * (1.0 / (half * frames))
+            out_ref[subject * half * frames : (subject + 1) * half * frames, lanes] = (
+                block - mean
+            ).astype(out_ref.dtype)
+
+
+def smooth(cells, weights, planes_at, runs_at, gram, sizes, depth, frames, extent, own, rim):
     vmem = pl.BlockSpec(memory_space=pltpu.VMEM)
     smem = pl.BlockSpec(memory_space=pltpu.SMEM)
+    groups = sizes[0] * sizes[1]
+    runs = own // groups
+    piece = gram.shape[4:]
+    rim_shape = pltpu.VMEM((rim, frames, RUN), jnp.bfloat16)
     return pl.pallas_call(
-        functools.partial(smooth_kernel, depth, frames, own, rim),
+        functools.partial(smooth_kernel, sizes, depth, frames, own, rim),
         out_shape=(
-            jax.ShapeDtypeStruct((own, frames, RUN), jnp.float32),
-            jax.ShapeDtypeStruct((rim, frames, RUN), jnp.bfloat16),
-            jax.ShapeDtypeStruct((rim, frames, RUN), jnp.bfloat16),
+            jax.ShapeDtypeStruct((groups * frames, runs * RUN), jnp.bfloat16),
+            jax.ShapeDtypeStruct(tuple(sizes[2:]) + piece, jnp.bfloat16),
         ),
-        in_specs=[smem, smem, vmem, vmem],
-        out_specs=(vmem, vmem, vmem),
-        scratch_shapes=[pltpu.VMEM((extent // RUN, depth * frames, RUN), jnp.float32)],
-        compiler_params=pltpu.CompilerParams(vmem_limit_bytes=48 * 1024 * 1024),
-    )(planes_at, runs_at, cells, weights)
+        in_specs=[smem, smem, vmem, vmem, vmem],
+        out_specs=(vmem, vmem),
+        scratch_shapes=[
+            pltpu.VMEM((extent // RUN * depth, frames, RUN), jnp.float32),
+            pltpu.VMEM(tuple(sizes[2:]) + piece, jnp.bfloat16),
+            rim_shape, rim_shape, rim_shape, rim_shape,
+            pltpu.VMEM((own, frames, RUN), jnp.bfloat16),
+            pltpu.VMEM((groups, runs, frames, RUN), jnp.bfloat16),
+            pltpu.SemaphoreType.DMA((2,)),
+            pltpu.SemaphoreType.DMA((2,)),
+            pltpu.SemaphoreType.DMA((groups,)),
+            pltpu.SemaphoreType.DMA((groups,)),
+        ]
+        + stage_sems(sizes)
+        + stage_scratch(sizes, piece),
+        compiler_params=pltpu.CompilerParams(
+            collective_id=2, has_side_effects=True, vmem_limit_bytes=60 * 1024 * 1024
+        ),
+    )(planes_at, runs_at, cells, weights, gram)
+
+
+def sum_kernel(sizes, part_ref, out_ref, full, s_send, s_recv, g_send, g_recv, *bufs):
+    at = coordinates(sizes)
+    barrier, count = greet_all(sizes)
+    pl.semaphore_wait(barrier, count)
+    for stage in scatter_stages(sizes, part_ref, bufs, full.at[tuple(at)], (s_send, s_recv)):
+        stage.start()
+        stage.finish()
+    for axis in range(4):
+        stage = Gather(sizes, axis, full, 0, (g_send, g_recv))
+        stage.start()
+        stage.finish()
+    out_ref[...] = full[...]
+
+
+def sum_over_all(part, sizes):
+    piece = part.shape[4:]
+    vmem = pl.BlockSpec(memory_space=pltpu.VMEM)
+    return pl.pallas_call(
+        functools.partial(sum_kernel, sizes),
+        out_shape=jax.ShapeDtypeStruct(part.shape, part.dtype),
+        in_specs=[vmem],
+        out_specs=vmem,
+        scratch_shapes=[pltpu.VMEM(part.shape, part.dtype)]
+        + stage_sems(sizes)
+        + stage_scratch(sizes, piece),
+        compiler_params=pltpu.CompilerParams(collective_id=3, has_side_effects=True),
+    )(part)
 
 
 def body(raw_frames, mask_index, subspace, rotation):
@@ -178,6 +443,7 @@
     per_device = subspace.shape[1]
     group_count = lax.axis_size("grp")
     slab_count = lax.axis_size("slab")
+    sizes = axes_of(group_count, slab_count)
     masked = per_device * slab_count * group_count
     frame_count = frames_here * group_count
     subject_frames = frame_count // 2
@@ -188,15 +454,7 @@
     runs_here = per_device // RUN
     own = runs_here * group_count
     rim = own * RAD // slab_depth
-    both = ("slab", "grp")
-
-    basis_part = lax.dot_general(
-        subspace, subspace, (((1,), (1,)), ((), ())), preferred_element_type=jnp.float32
-    ).astype(jnp.bfloat16)
-    basis_rows = lax.psum_scatter(
-        jnp.pad(basis_part, ((0, frame_count), (0, 0))), "grp", scatter_dimension=0, tiled=True
-    )
-    basis_rows = lax.psum(basis_rows.astype(jnp.float32), "slab")
+    across = (((1,), (1,)), ((), ()))
 
     starts = exchange(mask_index.reshape(runs_here, RUN), False, 1)[:, :, 0]
     starts = starts.reshape(slab_count, own) - slab * (slab_depth * extent)
@@ -209,43 +467,36 @@
     )
     planes_at = jnp.floor_divide(wanted, extent)
     runs_at = (wanted - planes_at * extent) // RUN
+    planes = planes_at[:, None] + jnp.arange(-RAD, RAD + 1, dtype=jnp.int32)[None, :]
+    taps = jnp.asarray(tap_weights(), jnp.float32)[None, :]
+    weight_at = jnp.where((planes >= 0) & (planes < slab_depth), taps, 0.0).reshape(-1)
+    cell_at = runs_at[:, None] * slab_depth + jnp.clip(planes, 0, slab_depth - 1)
+    cell_at = cell_at.reshape(-1)
+
+    basis_part = lax.dot_general(
+        subspace, subspace, across, preferred_element_type=jnp.float32
+    ).astype(jnp.bfloat16)
+    share = -(-rows_here // (16 * slab_count)) * 16
+    basis_part = jnp.pad(basis_part, ((0, frame_count), (0, 0))).reshape(group_count, rows_here, K)
+    basis_part = jnp.pad(basis_part, ((0, 0), (0, share * slab_count - rows_here), (0, 0)))
+    basis_part = basis_part.reshape(tuple(sizes) + (share, K))
 
     cells = jnp.pad(
         raw_frames.transpose(1, 0, 2), ((0, 0), (0, 0), (LEFT, SPAN - WIDE - LEFT))
     ).reshape(slab_depth * frames_here, -1)
-    inner, upward, downward = smooth(
-        cells, jnp.asarray(plane_weights()), planes_at, runs_at,
-        slab_depth, frames_here, extent, own, rim,
+    centered, basis_rows = smooth(
+        cells, jnp.asarray(plane_weights()), weight_at, cell_at, basis_part,
+        sizes, slab_depth, frames_here, extent, own, rim,
     )
-    ends = slab_count - 1
-    from_below = lax.ppermute(upward, "slab", [(i, i + 1) for i in range(ends)])
-    from_above = lax.ppermute(downward, "slab", [(i + 1, i) for i in range(ends)])
-    smoothed = jnp.concatenate(
-        [
-            inner[:rim] + from_below.astype(jnp.float32),
-            inner[rim : own - rim],
-            inner[own - rim :] + from_above.astype(jnp.float32),
-        ]
+    basis_rows = basis_rows.reshape(share * slab_count, K)[:rows_here].astype(jnp.float32)
+
+    stacked = jnp.concatenate([subspace, centered], 0)
+    data_part = lax.dot_general(
+        centered, stacked, across, preferred_element_type=jnp.float32
     ).astype(jnp.bfloat16)
-    regrouped = lax.all_to_all(smoothed, "grp", split_axis=0, concat_axis=0, tiled=True)
-    halves = (
-        regrouped.reshape(group_count, runs_here, frames_here, RUN)
-        .transpose(0, 2, 1, 3)
-        .reshape(2, subject_frames, per_device)
-        .astype(jnp.float32)
-    )
-    centered = (halves - jnp.mean(halves, axis=1, keepdims=True)).astype(jnp.bfloat16)
-    widened = centered.astype(jnp.float32)
-    squares = jnp.sum(widened * widened, axis=(1, 2))
-    power = exchange(jnp.broadcast_to(jnp.pad(squares, (0, 6))[:, None], (8, RUN)), True, 2)[:2, 0]
-    centered = centered.reshape(frame_count, per_device)
-    stacked = jnp.concatenate([subspace, centered], 0)
-    data_part = lax.psum(
-        lax.dot_general(
-            stacked, centered, (((1,), (1,)), ((), ())), preferred_element_type=jnp.float32
-        ),
-        both,
-    )
+    data_part = data_part.reshape(tuple(sizes) + (-1, order_rows))
+    data = sum_over_all(data_part, sizes).reshape(frame_count, order_rows).astype(jnp.float32)
+    power = jnp.sum(jnp.diagonal(data[:, K:]).reshape(2, subject_frames), axis=1)
     scales = lax.rsqrt(power / (masked * subject_frames) + epsilon)
     row_scale = jnp.concatenate([jnp.ones((K,), jnp.float32), jnp.repeat(scales, subject_frames)])
 
@@ -254,8 +505,8 @@
         turned, stacked, (((0,), (0,)), ((), ())), preferred_element_type=jnp.float32
     ).astype(jnp.bfloat16)
 
-    right = lax.dynamic_slice_in_dim(data_part, first_row, rows_here, 0)
-    low = jnp.pad(data_part[:K].T, ((rows_here, rows_here), (0, 0)))
+    right = lax.dynamic_slice_in_dim(data, first_row, rows_here, 1).T
+    low = jnp.pad(data[:, :K], ((rows_here, rows_here), (0, 0)))
     low = lax.dynamic_slice_in_dim(low, jnp.maximum(first_row - K + rows_here, 0), rows_here, 0)
     owned = jnp.concatenate([basis_rows + low, right], 1)
     owned_scale = lax.dynamic_slice_in_dim(row_scale, first_row, rows_here, 0)

time: 425 us -> 198 us (0.47)
  waiting for transfers between devices: 277 us -> 0 us
  Pallas kernels: 47.9 us -> 133 us
  blocking collectives: 27.8 us -> 0 us
  local copies, waits for them, and re-layouts: 16.4 us -> 33 us
  between operations: 14.6 us -> 0.82 us
  other arithmetic: 11.9 us -> 7.5 us
    unnamed x4 -> x0, waiting for transfers between devices: 145 us -> none
    psum x2 -> x0, waiting for transfers between devices: 130 us -> none  [the longest x1 92.3 us: body(): lax.psum(lax.dot_general(stacked, centered, (((1,), (1,)), ((), ())), pre...]
    pallas_call x1 -> x2, Pallas kernels: 20.2 us -> 117 us  [the longest x1 80.9 us: smooth(): pl.pallas_call(functools.partial(smooth_kernel, sizes, depth, frames, own...]
    all_to_all x1 -> x0, blocking collectives: 27.8 us -> none  [body(): lax.all_to_all(smoothed, 'grp', split_axis=0, concat_axis=0, tiled=True)]
    pallas_call x2 -> x1, Pallas kernels: 27.7 us -> 15.4 us  [exchange(): pl.pallas_call(functools.partial(exchange_kernel, total, groups, summed),...]
    unnamed x8, local copies, waits for them, and re-layouts: 2.43 us -> 9.09 us
    pad x1, local copies, waits for them, and re-layouts: 0.01 us -> 4.33 us  [body(): jnp.pad(basis_part, ((0, 0), (0, share * slab_count - rows_here), (0, 0)))]
  transfers between devices with their start and end apart: 5 -> 0, of which waited for: 4 -> 0; matrix products, arithmetic and copies ran while one was open for 7% -> 0% of each run, Pallas kernels for 3% -> 0%
where the time goes in v2:
time: 198 us; the launch traced here: 197 us
  Pallas kernels  133 us (67%)
  local copies, waits for them, and re-layouts  33 us (17%)
  matrix products  23.7 us (12%)
  other arithmetic  7.5 us (4%)
    pallas_call x1, Pallas kernels, smooth(): pl.pallas_call(functools.partial(smooth_kernel, sizes, depth, frames, own...  80.9 us
    pallas_call x1, Pallas kernels, sum_over_all(): pl.pallas_call(functools.partial(sum_kernel, sizes), out_shape=jax.ShapeD...  36.2 us
    pallas_call x1, Pallas kernels, exchange(): pl.pallas_call(functools.partial(exchange_kernel, total, groups, summed),...  15.4 us
    dot_general x1, matrix products, body(): lax.dot_general(turned, stacked, (((0,), (0,)), ((), ())), preferred_elem...  11.6 us
    dot_general x1, matrix products, body(): lax.dot_general(subspace, subspace, across, preferred_element_type=jnp.fl...  10.5 us
    unnamed x8, local copies, waits for them, and re-layouts  9.09 us
    pad x1, local copies, waits for them, and re-layouts, body(): jnp.pad(raw_frames.transpose(1, 0, 2), ((0, 0), (0, 0), (LEFT, SPAN - WID...  7.53 us
    pad x1, local copies, waits for them, and re-layouts, body(): jnp.pad(basis_part, ((0, 0), (0, share * slab_count - rows_here), (0, 0)))  4.33 us

profile of v2, /device:TPU:0, one launch (start us, length us, event | category | flops | bytes accessed | tf_op | source)
XLA Modules:
  0.0 197.5 jit_solution(10504118416570421764)
XLA Ops:
  0.6 15.4 %shard_map.77 = s32[32,14,128]{2,1,0:T(8,128)} custom-call(s32[14,128]{1,0:T(8,128)} %bitcast.33), custom_call_target="tpu_custom_call" | custom-call | tf_op jit(solution)/shard_map/pallas_call | solution.py:101
  16.1 1.6 subtract_reduce_fusion
  17.6 0.1 sub.32
  17.7 0.1 slice_bitcast_fusion
  17.8 0.1 fusion.6
  17.9 0.1 fusion.3
  18.0 0.8 add.100.r_ref
  18.8 0.7 fusion.5
  19.6 0.8 select_n.48.z_ref
  20.4 10.5 %convolution_convert_fusion.1 = bf16[1200,1200]{0,1:T(8,128)(2,1)} fusion(bf16[1200,1792]{1,0:T(8,128)(2,1)} %param.8), kind=kOutput, calls=%fused_computation.2 | convolution fusion | flops 5162399744 | bytes 7180800 | tf_op jit(solution)/shard_map/dot_general | solution.py:476
  30.9 4.2 %copy.17 = bf16[1200,1200]{1,0:T(8,128)(2,1)S(1)} copy(bf16[1200,1200]{0,1:T(8,128)(2,1)} %convolution_convert_fusion.1) | data formatting | bytes 5760000
  35.1 2.1 %pad.18.clone = bf16[1456,1200]{1,0:T(8,128)(2,1)} pad(bf16[1200,1200]{1,0:T(8,128)(2,1)S(1)} %copy.17, bf16[]{:T(256)} %constant.81.clone.1), padding=0_256x0_0 | pad | bytes 6374402 | tf_op jit(solution)/shard_map/jit(_pad)/pad | solution.py:480
  37.3 3.9 %reshape.212 = bf16[8,182,1200]{2,1,0:T(8,128)(2,1)} reshape(bf16[1456,1200]{1,0:T(8,128)(2,1)} %pad.18.clone) | data formatting | bytes 6988800 | tf_op jit(solution)/shard_map/reshape | solution.py:480
  41.1 4.3 %pad.19 = bf16[8,192,1200]{2,1,0:T(8,128)(2,1)} pad(bf16[8,182,1200]{2,1,0:T(8,128)(2,1)} %reshape.212, bf16[]{:T(256)} %constant.81.clone.1), padding=0_0x0_10x0_0 | pad | bytes 7180802 | tf_op jit(solution)/shard_map/jit(_pad)/pad | solution.py:481
  45.5 7.5 %pad.17 = bf16[12,32,11520]{2,1,0:T(8,128)(2,1)} pad(bf16[12,32,10752]{2,1,0:T(8,128)(2,1)} %bitcast.30, bf16[]{:T(256)} %constant.81.clone.1), padding=0_0x0_0x384_384 | pad | bytes 17104898 | tf_op jit(solution)/shard_map/jit(_pad)/pad | solution.py:484
  53.0 80.9 %shard_map.78 = (bf16[256,1792]{1,0:T(8,128)(2,1)}, bf16[2,2,48,1200]{3,2,1,0:T(8,128)(2,1)}) custom-call(f32[1176]{0:T(1024)} %select_n.48.z_ref, s32[1176]{0:T(1024)} %add.100.r_ref, bf16[384,11520]{1,0:T(8,128)(2,1)} %bitcast.27, bf16[3,1024,256]{2,1,0:T(8,128)(2,1)} %constant.91.clone.w_ref, bf16[4,2,2,2,48,1200]{5,4,3,2,1,0:T(8,128)(2,1)} %bitcast.29), custom_call_target="tpu_custom_call" | custom-call | tf_op jit(solution)/shard_map/pallas_call | solution.py:385
  133.9 0.0 copy-start.1
  133.9 2.6 %constant_dynamic-update-slice_fusion.1 = bf16[1456,1792]{1,0:T(8,128)(2,1)S(1)} fusion(bf16[1200,1792]{1,0:T(8,128)(2,1)} %param.8), kind=kLoop, calls=%fused_computation.20 | loop fusion | bytes 8601600
  136.5 0.0 copy-done.1
  136.5 0.1 constant_dynamic-update-slice_fusion
  136.6 0.0 copy-start
  136.6 2.3 %copy-done = bf16[1456,1792]{1,0:T(8,128)(2,1)} copy-done((bf16[1456,1792]{1,0:T(8,128)(2,1)}, bf16[1456,1792]{1,0:T(8,128)(2,1)S(1)}, u32[]{:S(2)}) %copy-start) | copy-done | bytes 5218328
  138.9 1.6 convolution_convert_fusion.2
  140.5 1.2 copy.15
  141.7 36.2 %shard_map.79 = bf16[4,2,2,2,8,1456]{5,4,3,2,1,0:T(8,128)(2,1)} custom-call(bf16[4,2,2,2,8,1456]{5,4,3,2,1,0:T(8,128)(2,1)} %bitcast.31), custom_call_target="tpu_custom_call" | custom-call | tf_op jit(solution)/shard_map/pallas_call | solution.py:429
  177.8 1.3 bitcast_convert_fusion
  179.1 0.1 slice.30
  179.3 2.3 %gather_fusion = f32[256]{0:T(256)S(1)} fusion(f32[256,256]{1,0:T(8,128)S(1)} %slice.30, s32[256]{0:T(256)S(1)} %bitcast.28), kind=kCustom, calls=%fused_computation | custom fusion | bytes 4096 | tf_op jit(solution)/shard_map/jit(diagonal)/cond/branch_0_fun/gather | solution.py:499
  181.6 0.1 bitcast_reduce_fusion
  181.8 0.1 broadcast_bitcast_fusion
  181.8 0.1 concatenate.49
  181.9 0.0 copy-start.2
  181.9 11.6 %convolution_convert_fusion = bf16[1200,1792]{1,0:T(8,128)(2,1)} fusion(bf16[1456,1792]{1,0:T(8,128)(2,1)} %copy-done, bf16[1456,1200]{0,1:T(8,128)(2,1)} %param.9, f32[1456]{0:T(1024)S(1)} %concatenate.49), kind=kOutput, calls=%fused_computation.1 | convolution fusion | flops 6269357056 | bytes 13019328 | tf_op jit(solution)/shard_map/dot_general | solution.py:504
  193.5 0.1 slice.29
  193.6 0.0 copy-done.2
  193.6 1.1 fusion.2
  194.7 0.1 dynamic-slice_bitcast_fusion
  194.9 0.1 copy.16
  195.0 0.1 pad_dynamic-slice_fusion.1
  195.1 2.4 %fusion.1 = f32[182,1456]{1,0:T(8,128)} fusion(f32[182,256]{1,0:T(8,128)S(1)} %copy.16, f32[182,1200]{1,0:T(8,128)} %fusion.2, f32[1456]{0:T(1024)S(1)} %concatenate.49, f32[182]{0:T(256)S(1)} %pad_dynamic-slice_fusion.1), kind=kLoop, calls=%fused_computation.8 | loop fusion | flops 1059968 | bytes 2126488 | tf_op jit(solution)/shard_map/div | solution.py:513
  (4 shorter events, 0.0 us)
Async XLA Ops:
  133.9 2.6 %copy-start.1 = (bf16[256,1792]{1,0:T(8,128)(2,1)S(1)}, bf16[256,1792]{1,0:T(8,128)(2,1)}, u32[]{:S(2)}) copy-start(bf16[256,1792]{1,0:T(8,128)(2,1)} %get-tuple-element.5) | copy-start | bytes 2752516
  136.6 2.3 %copy-start = (bf16[1456,1792]{1,0:T(8,128)(2,1)}, bf16[1456,1792]{1,0:T(8,128)(2,1)S(1)}, u32[]{:S(2)}) copy-start(bf16[1456,1792]{1,0:T(8,128)(2,1)S(1)} %constant_dynamic-update-slice_fusion) | copy-start | bytes 15654916
  181.9 11.7 %copy-start.2 = (bf16[2,2,48,1200]{3,2,1,0:T(8,128)(2,1)S(1)}, bf16[2,2,48,1200]{3,2,1,0:T(8,128)(2,1)}, u32[]{:S(2)}) copy-start(bf16[2,2,48,1200]{3,2,1,0:T(8,128)(2,1)} %get-tuple-element.4) | copy-start | bytes 1382404

commit v3 on v2

--- a/solution.py
+++ b/solution.py
@@ -149,13 +149,15 @@
 
 
 class Scatter:
-    def __init__(self, sizes, axis, src, landed, out, sems):
+    def __init__(self, sizes, axis, left, src, landed, out, sems):
         self.sizes, self.axis, self.src, self.landed, self.out = sizes, axis, src, landed, out
+        self.dim = left.index(axis)
+        self.left = [other for other in left if other != axis]
         self.send_sem, self.recv_sem = sems
         self.at = coordinates(sizes)
 
     def part(self, where):
-        return self.src.at[(slice(None),) * self.axis + (where,)]
+        return self.src.at[(slice(None),) * self.dim + (where,)]
 
     def copy(self, step):
         there, other = moved(self.at, self.sizes, self.axis, step)
@@ -176,7 +178,7 @@
         for step in range(1, self.sizes[self.axis]):
             self.copy(step).wait()
         mine = self.part(self.at[self.axis])
-        lead = self.sizes[: self.axis]
+        lead = [self.sizes[axis] for axis in self.left]
         total = math.prod(lead)
 
         def add(index, _):
@@ -221,12 +223,17 @@
             self.copy(step).wait()
 
 
+STAGES = (3, 1, 2, 0)
+
+
 def stage_scratch(sizes, piece):
     out = []
-    for axis in range(3, -1, -1):
-        shape = tuple(sizes[:axis]) + piece
+    left = [0, 1, 2, 3]
+    for axis in STAGES:
+        left.remove(axis)
+        shape = tuple(sizes[other] for other in left) + piece
         out.append(pltpu.VMEM((sizes[axis] - 1,) + shape, jnp.bfloat16))
-        if axis:
+        if left:
             out.append(pltpu.VMEM(shape, jnp.bfloat16))
     return out
 
@@ -238,10 +245,12 @@
 
 def scatter_stages(sizes, src, bufs, result, sems):
     stages = []
-    for number, axis in enumerate(range(3, -1, -1)):
-        landed = bufs[2 * number]
-        out = bufs[2 * number + 1] if axis else result
-        stages.append(Scatter(sizes, axis, src, landed, out, sems))
+    left = [0, 1, 2, 3]
+    for number, axis in enumerate(STAGES):
+        last = number == len(STAGES) - 1
+        out = result if last else bufs[2 * number + 1]
+        stages.append(Scatter(sizes, axis, left, src, bufs[2 * number], out, sems))
+        left = stages[-1].left
         src = out
     return stages
 
@@ -456,7 +465,8 @@
     rim = own * RAD // slab_depth
     across = (((1,), (1,)), ((), ()))
 
-    starts = exchange(mask_index.reshape(runs_here, RUN), False, 1)[:, :, 0]
+    starts = jnp.pad(mask_index.reshape(runs_here, RUN)[:, 0], (0, RUN - runs_here))
+    starts = exchange(starts.reshape(1, RUN), False, 1)[:, 0, :runs_here]
     starts = starts.reshape(slab_count, own) - slab * (slab_depth * extent)
     wanted = jnp.concatenate(
         [
@@ -473,12 +483,16 @@
     cell_at = runs_at[:, None] * slab_depth + jnp.clip(planes, 0, slab_depth - 1)
     cell_at = cell_at.reshape(-1)
 
+    share = -(-rows_here // (16 * slab_count)) * 16
+    spread = []
+    for group in range(group_count):
+        begin, end = (min(K, (group + more) * rows_here) for more in (0, 1))
+        spread.append(
+            jnp.pad(subspace[begin:end], ((0, share * slab_count - (end - begin)), (0, 0)))
+        )
     basis_part = lax.dot_general(
-        subspace, subspace, across, preferred_element_type=jnp.float32
+        jnp.concatenate(spread), subspace, across, preferred_element_type=jnp.float32
     ).astype(jnp.bfloat16)
-    share = -(-rows_here // (16 * slab_count)) * 16
-    basis_part = jnp.pad(basis_part, ((0, frame_count), (0, 0))).reshape(group_count, rows_here, K)
-    basis_part = jnp.pad(basis_part, ((0, 0), (0, share * slab_count - rows_here), (0, 0)))
     basis_part = basis_part.reshape(tuple(sizes) + (share, K))
 
     cells = jnp.pad(

time: 198 us -> 178 us (0.90)
  Pallas kernels: 133 us -> 118 us
  local copies, waits for them, and re-layouts: 33 us -> 29.4 us
  matrix products: 23.7 us -> 21.5 us
    pallas_call x1, Pallas kernels: 80.9 us -> 69.4 us  [smooth(): pl.pallas_call(functools.partial(smooth_kernel, sizes, depth, frames, own...]
    pad x2 -> x0, local copies, waits for them, and re-layouts: 6.47 us -> none  [the longest x1 4.33 us: body(): jnp.pad(basis_part, ((0, 0), (0, share * slab_count - rows_here), (0, 0)))]
    convert_element_type x0 -> x1, local copies, waits for them, and re-layouts: none -> 5.99 us  [body(): basis_part = lax.dot_general(jnp.concatenate(spread), subspace, across, p...]
    pallas_call x1, Pallas kernels: 15.4 us -> 11.6 us  [exchange(): pl.pallas_call(functools.partial(exchange_kernel, total, groups, summed),...]
    slice x0 -> x3, local copies, waits for them, and re-layouts: none -> 3.58 us  [the longest x2 2.77 us: body(): subspace[begin:end]]
    unnamed x8 -> x17, local copies, waits for them, and re-layouts: 9.09 us -> 5.72 us
    reshape x1, local copies, waits for them, and re-layouts: 3.88 us -> 0.52 us  [body(): starts = exchange(starts.reshape(1, RUN), False, 1)[:, 0, :runs_here]]
    dot_general x1, matrix products: 10.5 us -> 8.32 us  [body(): lax.dot_general(jnp.concatenate(spread), subspace, across, preferred_elem...]
where the time goes in v3:
time: 178 us; the launch traced here: 177 us
  Pallas kernels  118 us (66%)
  local copies, waits for them, and re-layouts  29.4 us (17%)
  matrix products  21.5 us (12%)
  other arithmetic  6.89 us (4%)
    pallas_call x1, Pallas kernels, smooth(): pl.pallas_call(functools.partial(smooth_kernel, sizes, depth, frames, own...  69.4 us
    pallas_call x1, Pallas kernels, sum_over_all(): pl.pallas_call(functools.partial(sum_kernel, sizes), out_shape=jax.ShapeD...  37.4 us
    pallas_call x1, Pallas kernels, exchange(): pl.pallas_call(functools.partial(exchange_kernel, total, groups, summed),...  11.6 us
    dot_general x1, matrix products, body(): lax.dot_general(turned, stacked, (((0,), (0,)), ((), ())), preferred_elem...  11.6 us
    dot_general x1, matrix products, body(): lax.dot_general(jnp.concatenate(spread), subspace, across, preferred_elem...  8.32 us
    pad x1, local copies, waits for them, and re-layouts, body(): jnp.pad(raw_frames.transpose(1, 0, 2), ((0, 0), (0, 0), (LEFT, SPAN - WID...  7.53 us
    convert_element_type x1, local copies, waits for them, and re-layouts, body(): basis_part = lax.dot_general(jnp.concatenate(spread), subspace, across, p...  5.99 us
    unnamed x17, local copies, waits for them, and re-layouts  5.72 us

profile of v3, /device:TPU:0, one launch (start us, length us, event | category | flops | bytes accessed | tf_op | source)
XLA Modules:
  0.0 177.1 jit_solution(12503282060913937501)
XLA Ops:
  0.6 0.0 copy-start.4
  0.7 0.8 slice_reduce_fusion
  1.5 0.5 pad_bitcast_fusion.x_ref
  2.0 11.6 %shard_map.77 = s32[32,1,128]{2,1,0:T(1,128)} custom-call(s32[1,128]{1,0:T(1,128)} %pad_bitcast_fusion.x_ref), custom_call_target="tpu_custom_call" | custom-call | tf_op jit(solution)/shard_map/pallas_call | solution.py:101
  13.6 0.8 subtract_reduce_fusion
  14.3 0.1 sub.32
  14.4 0.1 slice_bitcast_fusion
  14.5 0.1 fusion.6
  14.6 0.1 fusion.3
  14.7 0.8 add.110.r_ref
  15.5 0.7 fusion.5
  16.3 0.8 select_n.48.z_ref
  17.1 0.0 copy-start
  17.1 2.7 %fusion.8 = (bf16[182,1792]{1,0:T(8,128)(2,1)S(1)}, bf16[182,1792]{1,0:T(8,128)(2,1)S(1)}, bf16[182,1792]{1,0:T(8,128)(2,1)S(1)}, bf16[182,1792]{1,0:T(8,128)(2,1)S(1)}, bf16[182,1792]{1,0:T(8,128)(2,1)S(1)}) fusion(bf16[1200,1792]{1,0:T(8,128)(2,1)} %param.8), kind=kLoop, calls=%fused_computation.50 | loop fusion | bytes 6522880 | tf_op jit(solution)/shard_map/slice | solution.py:491
  19.8 0.0 copy-done.4
  19.8 0.5 copy-done
  20.3 0.2 select_dynamic-update-slice_fusion
  20.8 0.1 slice.55
  21.0 8.3 %convolution_convert_fusion = bf16[1536,1200]{0,1:T(8,128)(2,1)} fusion(bf16[1536,1792]{1,0:T(8,128)(2,1)S(1)} %broadcast_dynamic-update-slice_fusion, bf16[1200,1792]{1,0:T(8,128)(2,1)S(1)} %copy-done), kind=kOutput, calls=%fused_computation.1 | convolution fusion | flops 6607872000 | bytes 13492224 | tf_op jit(solution)/shard_map/dot_general | solution.py:493
  29.3 6.0 %copy.17 = bf16[1536,1200]{1,0:T(8,128)(2,1)} copy(bf16[1536,1200]{0,1:T(8,128)(2,1)} %convolution_convert_fusion) | data formatting | bytes 7372800 | tf_op jit(solution)/shard_map/convert_element_type | solution.py:495
  35.3 7.5 %pad.39 = bf16[12,32,11520]{2,1,0:T(8,128)(2,1)} pad(bf16[12,32,10752]{2,1,0:T(8,128)(2,1)} %bitcast.32, bf16[]{:T(256)} %constant.83.clone.1), padding=0_0x0_0x384_384 | pad | bytes 17104898 | tf_op jit(solution)/shard_map/jit(_pad)/pad | solution.py:498
  42.8 69.4 %shard_map.78 = (bf16[256,1792]{1,0:T(8,128)(2,1)}, bf16[2,2,48,1200]{3,2,1,0:T(8,128)(2,1)}) custom-call(f32[1176]{0:T(1024)} %select_n.48.z_ref, s32[1176]{0:T(1024)} %add.110.r_ref, bf16[384,11520]{1,0:T(8,128)(2,1)} %bitcast.29, bf16[3,1024,256]{2,1,0:T(8,128)(2,1)} %constant.94.clone.w_ref, bf16[4,2,2,2,48,1200]{5,4,3,2,1,0:T(8,128)(2,1)} %bitcast.31), custom_call_target="tpu_custom_call" | custom-call | tf_op jit(solution)/shard_map/pallas_call | solution.py:394
  112.3 0.0 copy-start.2
  112.3 2.6 %constant_dynamic-update-slice_fusion.1 = bf16[1456,1792]{1,0:T(8,128)(2,1)S(1)} fusion(bf16[1200,1792]{1,0:T(8,128)(2,1)} %param.8), kind=kLoop, calls=%fused_computation.27 | loop fusion | bytes 8601600
  114.9 0.0 copy-done.2
  114.9 0.1 constant_dynamic-update-slice_fusion
  115.0 0.0 copy-start.1
  115.0 2.3 %copy-done.1 = bf16[1456,1792]{1,0:T(8,128)(2,1)} copy-done((bf16[1456,1792]{1,0:T(8,128)(2,1)}, bf16[1456,1792]{1,0:T(8,128)(2,1)S(1)}, u32[]{:S(2)}) %copy-start.1) | copy-done | bytes 5218328
  117.3 1.6 convolution_convert_fusion.2
  118.8 1.2 copy.18
  120.0 37.4 %shard_map.79 = bf16[4,2,2,2,8,1456]{5,4,3,2,1,0:T(8,128)(2,1)} custom-call(bf16[4,2,2,2,8,1456]{5,4,3,2,1,0:T(8,128)(2,1)} %bitcast.33), custom_call_target="tpu_custom_call" | custom-call | tf_op jit(solution)/shard_map/pallas_call | solution.py:438
  157.4 1.3 bitcast_convert_fusion
  158.7 0.1 slice.64
  158.9 2.3 %gather_fusion = f32[256]{0:T(256)S(1)} fusion(f32[256,256]{1,0:T(8,128)S(1)} %slice.64, s32[256]{0:T(256)S(1)} %bitcast.30), kind=kCustom, calls=%fused_computation | custom fusion | bytes 4096 | tf_op jit(solution)/shard_map/jit(diagonal)/cond/branch_0_fun/gather | solution.py:513
  161.2 0.1 bitcast_reduce_fusion
  161.4 0.1 broadcast_bitcast_fusion
  161.4 0.1 concatenate.53
  161.5 0.0 copy-start.3
  161.5 11.6 %convolution_convert_fusion.1 = bf16[1200,1792]{1,0:T(8,128)(2,1)} fusion(bf16[1456,1792]{1,0:T(8,128)(2,1)} %copy-done.1, bf16[1456,1200]{0,1:T(8,128)(2,1)} %param.9, f32[1456]{0:T(1024)S(1)} %concatenate.53), kind=kOutput, calls=%fused_computation.2 | convolution fusion | flops 6269357056 | bytes 13019328 | tf_op jit(solution)/shard_map/dot_general | solution.py:518
  173.1 0.1 slice.63
  173.2 0.0 copy-done.3
  173.2 1.1 fusion.2
  174.3 0.1 dynamic-slice_bitcast_fusion
  174.5 0.1 copy.19
  174.6 0.1 pad_dynamic-slice_fusion.1
  174.7 2.4 %fusion.1 = f32[182,1456]{1,0:T(8,128)} fusion(f32[182,256]{1,0:T(8,128)S(1)} %copy.19, f32[182,1200]{1,0:T(8,128)} %fusion.2, f32[1456]{0:T(1024)S(1)} %concatenate.53, f32[182]{0:T(256)S(1)} %pad_dynamic-slice_fusion.1), kind=kLoop, calls=%fused_computation.8 | loop fusion | flops 1059968 | bytes 2126488 | tf_op jit(solution)/shard_map/div | solution.py:527
  (11 shorter events, 0.4 us)
Async XLA Ops:
  0.6 19.1 %copy-start.4 = (pred[192]{0:T(512)(128)(4,1)S(1)}, pred[192]{0:T(512)(128)(4,1)}, u32[]{:S(2)}) copy-start(pred[192]{0:T(512)(128)(4,1)} %constant.84.clone.1) | copy-start | bytes 580
  17.1 3.2 %copy-start = (bf16[1200,1792]{1,0:T(8,128)(2,1)S(1)}, bf16[1200,1792]{1,0:T(8,128)(2,1)}, u32[]{:S(2)}) copy-start(bf16[1200,1792]{1,0:T(8,128)(2,1)} %param.8) | copy-start | bytes 12902404
  112.3 2.6 %copy-start.2 = (bf16[256,1792]{1,0:T(8,128)(2,1)S(1)}, bf16[256,1792]{1,0:T(8,128)(2,1)}, u32[]{:S(2)}) copy-start(bf16[256,1792]{1,0:T(8,128)(2,1)} %get-tuple-element.5) | copy-start | bytes 2752516
  115.0 2.3 %copy-start.1 = (bf16[1456,1792]{1,0:T(8,128)(2,1)}, bf16[1456,1792]{1,0:T(8,128)(2,1)S(1)}, u32[]{:S(2)}) copy-start(bf16[1456,1792]{1,0:T(8,128)(2,1)S(1)} %constant_dynamic-update-slice_fusion) | copy-start | bytes 15654916
  161.5 11.7 %copy-start.3 = (bf16[2,2,48,1200]{3,2,1,0:T(8,128)(2,1)S(1)}, bf16[2,2,48,1200]{3,2,1,0:T(8,128)(2,1)}, u32[]{:S(2)}) copy-start(bf16[2,2,48,1200]{3,2,1,0:T(8,128)(2,1)} %get-tuple-element.4) | copy-start | bytes 1382404

commit v4 on v3

--- a/solution.py
+++ b/solution.py
@@ -228,8 +228,10 @@
 
 def stage_scratch(sizes, piece):
     out = []
-    left = [0, 1, 2, 3]
+    left = [axis for axis in range(4) if sizes[axis] > 1]
     for axis in STAGES:
+        if sizes[axis] == 1:
+            continue
         left.remove(axis)
         shape = tuple(sizes[other] for other in left) + piece
         out.append(pltpu.VMEM((sizes[axis] - 1,) + shape, jnp.bfloat16))
@@ -246,8 +248,13 @@
 def scatter_stages(sizes, src, bufs, result, sems):
     stages = []
     left = [0, 1, 2, 3]
-    for number, axis in enumerate(STAGES):
-        last = number == len(STAGES) - 1
+    for axis in STAGES:
+        if sizes[axis] == 1:
+            src = src.at[(slice(None),) * left.index(axis) + (0,)]
+            left = [other for other in left if other != axis]
+    order = [axis for axis in STAGES if sizes[axis] > 1]
+    for number, axis in enumerate(order):
+        last = number == len(order) - 1
         out = result if last else bufs[2 * number + 1]
         stages.append(Scatter(sizes, axis, left, src, bufs[2 * number], out, sems))
         left = stages[-1].left
@@ -332,22 +339,6 @@
         return 0
 
     lax.fori_loop(rim, own - rim, inner, 0)
-    halo_up.wait()
-    halo_down.wait()
-    low_part = jnp.where(slab > 0, 1.0, 0.0)
-    high_part = jnp.where(slab < slabs - 1, 1.0, 0.0)
-
-    def edge(run, _):
-        picked_ref[run] = (picked(run) + low_part * below[run].astype(jnp.float32)).astype(
-            picked_ref.dtype
-        )
-        last = run + own - rim
-        picked_ref[last] = (picked(last) + high_part * above[run].astype(jnp.float32)).astype(
-            picked_ref.dtype
-        )
-        return 0
-
-    lax.fori_loop(0, rim, edge, 0)
 
     def trade(step):
         other = lax.rem(grp + step, groups)
@@ -357,8 +348,33 @@
             device_id=(slab, other), device_id_type=MESH,
         )
 
-    for step in range(1, groups):
-        trade(step).start()
+    outer = -(-rim // runs)
+
+    def start_trades(at_rim):
+        for step in range(1, groups):
+            other = lax.rem(grp + step, groups)
+            inside = (other >= outer) & (other < groups - outer)
+            pl.when(jnp.logical_not(inside) if at_rim else inside)(trade(step).start)
+
+    start_trades(False)
+    halo_up.wait()
+    halo_down.wait()
+    low_part = jnp.where(slab > 0, 1.0, 0.0)
+    high_part = jnp.where(slab < slabs - 1, 1.0, 0.0)
+
+    def edge(run, _):
+        picked_ref[run] = (picked(run) + low_part * below[run].astype(jnp.float32)).astype(
+            picked_ref.dtype
+        )
+        last = run + own - rim
+        picked_ref[last] = (picked(last) + high_part * above[run].astype(jnp.float32)).astype(
+            picked_ref.dtype
+        )
+        return 0
+
+    lax.fori_loop(0, rim, edge, 0)
+
+    start_trades(True)
     regrouped[grp] = picked_ref[pl.ds(grp * runs, runs)]
 
     scatter[1].finish()
@@ -491,8 +507,8 @@
             jnp.pad(subspace[begin:end], ((0, share * slab_count - (end - begin)), (0, 0)))
         )
     basis_part = lax.dot_general(
-        jnp.concatenate(spread), subspace, across, preferred_element_type=jnp.float32
-    ).astype(jnp.bfloat16)
+        subspace, jnp.concatenate(spread), across, preferred_element_type=jnp.float32
+    ).T.astype(jnp.bfloat16)
     basis_part = basis_part.reshape(tuple(sizes) + (share, K))
 
     cells = jnp.pad(
@@ -506,11 +522,15 @@
 
     stacked = jnp.concatenate([subspace, centered], 0)
     data_part = lax.dot_general(
-        centered, stacked, across, preferred_element_type=jnp.float32
-    ).astype(jnp.bfloat16)
-    data_part = data_part.reshape(tuple(sizes) + (-1, order_rows))
-    data = sum_over_all(data_part, sizes).reshape(frame_count, order_rows).astype(jnp.float32)
-    power = jnp.sum(jnp.diagonal(data[:, K:]).reshape(2, subject_frames), axis=1)
+        stacked, centered, across, preferred_element_type=jnp.float32
+    ).T.astype(jnp.bfloat16)
+    flat = (1, group_count) + tuple(sizes[2:])
+    data_part = data_part.reshape(flat + (-1, order_rows))
+    data = sum_over_all(data_part, flat).reshape(frame_count, order_rows).astype(jnp.float32)
+    row = lax.broadcasted_iota(jnp.int32, data.shape, 0)
+    column = lax.broadcasted_iota(jnp.int32, data.shape, 1)
+    squares = jnp.sum(jnp.where(row + K == column, data, 0.0), axis=1)
+    power = jnp.sum(squares.reshape(2, subject_frames), axis=1)
     scales = lax.rsqrt(power / (masked * subject_frames) + epsilon)
     row_scale = jnp.concatenate([jnp.ones((K,), jnp.float32), jnp.repeat(scales, subject_frames)])
 

time: 178 us -> 173 us (0.972)
  local copies, waits for them, and re-layouts: 29.4 us -> 27 us
    pallas_call x1, Pallas kernels: 37.4 us -> 33.6 us  [sum_over_all(): pl.pallas_call(functools.partial(sum_kernel, sizes), out_shape=jax.ShapeD...]
    pallas_call x1, Pallas kernels: 69.4 us -> 72.4 us  [smooth(): pl.pallas_call(functools.partial(smooth_kernel, sizes, depth, frames, own...]
    gather x1 -> x0, local copies, waits for them, and re-layouts: 2.34 us -> none  [body(): jnp.diagonal(data[:, K:]).reshape(2, subject_frames)]
    unnamed x17 -> x20, local copies, waits for them, and re-layouts: 5.72 us -> 5.82 us
where the time goes in v4:
time: 173 us; the launch traced here: 172 us
  Pallas kernels  118 us (68%)
  local copies, waits for them, and re-layouts  27 us (16%)
  matrix products  21.5 us (12%)
  other arithmetic  5.24 us (3%)
    pallas_call x1, Pallas kernels, smooth(): pl.pallas_call(functools.partial(smooth_kernel, sizes, depth, frames, own...  72.4 us
    pallas_call x1, Pallas kernels, sum_over_all(): pl.pallas_call(functools.partial(sum_kernel, sizes), out_shape=jax.ShapeD...  33.6 us
    dot_general x1, matrix products, body(): lax.dot_general(turned, stacked, (((0,), (0,)), ((), ())), preferred_elem...  11.6 us
    pallas_call x1, Pallas kernels, exchange(): pl.pallas_call(functools.partial(exchange_kernel, total, groups, summed),...  11.6 us
    dot_general x1, matrix products, body(): lax.dot_general(subspace, jnp.concatenate(spread), across, preferred_elem...  8.32 us
    pad x1, local copies, waits for them, and re-layouts, body(): jnp.pad(raw_frames.transpose(1, 0, 2), ((0, 0), (0, 0), (LEFT, SPAN - WID...  7.52 us
    convert_element_type x1, local copies, waits for them, and re-layouts, body(): basis_part = lax.dot_general(subspace, jnp.concatenate(spread), across, p...  5.99 us
    unnamed x20, local copies, waits for them, and re-layouts  5.82 us

profile of v4, /device:TPU:0, one launch (start us, length us, event | category | flops | bytes accessed | tf_op | source)
XLA Modules:
  0.0 172.2 jit_solution(13509305013804065814)
XLA Ops:
  0.6 0.0 copy-start.5
  0.7 0.8 slice_reduce_fusion
  1.5 0.5 pad_bitcast_fusion.x_ref
  2.0 11.6 %shard_map.77 = s32[32,1,128]{2,1,0:T(1,128)} custom-call(s32[1,128]{1,0:T(1,128)} %pad_bitcast_fusion.x_ref), custom_call_target="tpu_custom_call" | custom-call | tf_op jit(solution)/shard_map/pallas_call | solution.py:101
  13.6 0.8 subtract_reduce_fusion
  14.3 0.1 sub.32
  14.4 0.1 slice_bitcast_fusion
  14.5 0.1 fusion.6
  14.6 0.1 fusion.3
  14.7 0.8 add.117.r_ref
  15.5 0.7 fusion.5
  16.3 0.8 select_n.49.z_ref
  17.1 0.0 copy-start
  17.1 2.7 %fusion.8 = (bf16[182,1792]{1,0:T(8,128)(2,1)S(1)}, bf16[182,1792]{1,0:T(8,128)(2,1)S(1)}, bf16[182,1792]{1,0:T(8,128)(2,1)S(1)}, bf16[182,1792]{1,0:T(8,128)(2,1)S(1)}, bf16[182,1792]{1,0:T(8,128)(2,1)S(1)}) fusion(bf16[1200,1792]{1,0:T(8,128)(2,1)} %param.8), kind=kLoop, calls=%fused_computation.49 | loop fusion | bytes 6522880 | tf_op jit(solution)/shard_map/slice | solution.py:507
  19.8 0.0 copy-done.5
  19.8 0.5 copy-done
  20.3 0.2 select_dynamic-update-slice_fusion
  20.8 0.1 slice.52
  21.0 8.3 %convolution_convert_fusion = bf16[1536,1200]{0,1:T(8,128)(2,1)} fusion(bf16[1536,1792]{1,0:T(8,128)(2,1)S(1)} %broadcast_dynamic-update-slice_fusion, bf16[1200,1792]{1,0:T(8,128)(2,1)S(1)} %copy-done), kind=kOutput, calls=%fused_computation | convolution fusion | flops 6607872000 | bytes 13492224 | tf_op jit(solution)/shard_map/dot_general | solution.py:509
  29.3 6.0 %copy.14 = bf16[1536,1200]{1,0:T(8,128)(2,1)} copy(bf16[1536,1200]{0,1:T(8,128)(2,1)} %convolution_convert_fusion) | data formatting | bytes 7372800 | tf_op jit(solution)/shard_map/convert_element_type | solution.py:511
  35.3 7.5 %pad.39 = bf16[12,32,11520]{2,1,0:T(8,128)(2,1)} pad(bf16[12,32,10752]{2,1,0:T(8,128)(2,1)} %bitcast.28, bf16[]{:T(256)} %constant.82.clone.1), padding=0_0x0_0x384_384 | pad | bytes 17104898 | tf_op jit(solution)/shard_map/jit(_pad)/pad | solution.py:514
  42.8 72.4 %shard_map.78 = (bf16[256,1792]{1,0:T(8,128)(2,1)}, bf16[2,2,48,1200]{3,2,1,0:T(8,128)(2,1)}) custom-call(f32[1176]{0:T(1024)} %select_n.49.z_ref, s32[1176]{0:T(1024)} %add.117.r_ref, bf16[384,11520]{1,0:T(8,128)(2,1)} %bitcast.25, bf16[3,1024,256]{2,1,0:T(8,128)(2,1)} %constant.97.clone.w_ref, bf16[4,2,2,2,48,1200]{5,4,3,2,1,0:T(8,128)(2,1)} %bitcast.27), custom_call_target="tpu_custom_call" | custom-call | tf_op jit(solution)/shard_map/pallas_call | solution.py:410
  115.2 0.0 copy-start.3
  115.2 2.6 %constant_dynamic-update-slice_fusion.1 = bf16[1456,1792]{1,0:T(8,128)(2,1)S(1)} fusion(bf16[1200,1792]{1,0:T(8,128)(2,1)} %param.8), kind=kLoop, calls=%fused_computation.26 | loop fusion | bytes 8601600
  117.8 0.0 copy-done.3
  117.8 0.1 constant_dynamic-update-slice_fusion
  117.9 0.0 copy-start.2
  117.9 2.3 %copy-done.2 = bf16[1456,1792]{1,0:T(8,128)(2,1)} copy-done((bf16[1456,1792]{1,0:T(8,128)(2,1)}, bf16[1456,1792]{1,0:T(8,128)(2,1)S(1)}, u32[]{:S(2)}) %copy-start.2) | copy-done | bytes 5218328
  120.2 1.6 convolution_convert_fusion.2
  121.8 1.2 copy.15
  123.0 33.6 %shard_map.79 = bf16[1,8,2,2,8,1456]{5,4,3,2,1,0:T(8,128)(2,1)} custom-call(bf16[1,8,2,2,8,1456]{5,4,3,2,1,0:T(8,128)(2,1)} %bitcast.29), custom_call_target="tpu_custom_call" | custom-call | tf_op jit(solution)/shard_map/pallas_call | solution.py:454
  156.6 1.5 select_reduce_fusion
  158.1 0.1 reduce_sum.21
  158.2 0.1 reduce_sum.22
  158.3 0.1 broadcast_bitcast_fusion
  158.4 0.1 concatenate.48
  158.5 0.0 copy-start.1
  158.5 0.0 copy-start.4
  158.5 11.6 %convolution_convert_fusion.1 = bf16[1200,1792]{1,0:T(8,128)(2,1)} fusion(bf16[1456,1792]{1,0:T(8,128)(2,1)} %copy-done.2, bf16[1456,1200]{0,1:T(8,128)(2,1)} %param.9, f32[1456]{0:T(1024)S(1)} %concatenate.48), kind=kOutput, calls=%fused_computation.1 | convolution fusion | flops 6269357056 | bytes 13019328 | tf_op jit(solution)/shard_map/dot_general | solution.py:538
  170.1 0.0 copy-done.1
  170.1 0.1 slice.57
  170.2 0.0 copy-done.4
  170.2 0.2 fusion.2
  170.4 0.2 bitcast_convert_fusion
  170.6 0.1 constant_dynamic-slice_fusion
  170.8 0.1 copy.17
  170.9 0.1 pad_dynamic-slice_fusion.1
  171.0 1.2 fusion.1
  (11 shorter events, 0.4 us)
Async XLA Ops:
  0.6 19.1 %copy-start.5 = (pred[192]{0:T(512)(128)(4,1)S(1)}, pred[192]{0:T(512)(128)(4,1)}, u32[]{:S(2)}) copy-start(pred[192]{0:T(512)(128)(4,1)} %constant.83.clone.1) | copy-start | bytes 580
  17.1 3.2 %copy-start = (bf16[1200,1792]{1,0:T(8,128)(2,1)S(1)}, bf16[1200,1792]{1,0:T(8,128)(2,1)}, u32[]{:S(2)}) copy-start(bf16[1200,1792]{1,0:T(8,128)(2,1)} %param.8) | copy-start | bytes 12902404
  115.2 2.6 %copy-start.3 = (bf16[256,1792]{1,0:T(8,128)(2,1)S(1)}, bf16[256,1792]{1,0:T(8,128)(2,1)}, u32[]{:S(2)}) copy-start(bf16[256,1792]{1,0:T(8,128)(2,1)} %get-tuple-element.5) | copy-start | bytes 2752516
  117.9 2.3 %copy-start.2 = (bf16[1456,1792]{1,0:T(8,128)(2,1)}, bf16[1456,1792]{1,0:T(8,128)(2,1)S(1)}, u32[]{:S(2)}) copy-start(bf16[1456,1792]{1,0:T(8,128)(2,1)S(1)} %constant_dynamic-update-slice_fusion) | copy-start | bytes 15654916
  158.5 11.6 %copy-start.1 = (bf16[1,8,2,2,8,1456]{5,4,3,2,1,0:T(8,128)(2,1)S(1)}, bf16[1,8,2,2,8,1456]{5,4,3,2,1,0:T(8,128)(2,1)}, u32[]{:S(2)}) copy-start(bf16[1,8,2,2,8,1456]{5,4,3,2,1,0:T(8,128)(2,1)} %shard_map.79) | copy-start | bytes 2236420
  158.5 11.7 %copy-start.4 = (bf16[2,2,48,1200]{3,2,1,0:T(8,128)(2,1)S(1)}, bf16[2,2,48,1200]{3,2,1,0:T(8,128)(2,1)}, u32[]{:S(2)}) copy-start(bf16[2,2,48,1200]{3,2,1,0:T(8,128)(2,1)} %get-tuple-element.4) | copy-start | bytes 1382404

commit v5 on v4

--- a/solution.py
+++ b/solution.py
@@ -357,6 +357,8 @@
             pl.when(jnp.logical_not(inside) if at_rim else inside)(trade(step).start)
 
     start_trades(False)
+    scatter[1].finish()
+    scatter[2].start()
     halo_up.wait()
     halo_down.wait()
     low_part = jnp.where(slab > 0, 1.0, 0.0)
@@ -377,10 +379,9 @@
     start_trades(True)
     regrouped[grp] = picked_ref[pl.ds(grp * runs, runs)]
 
-    scatter[1].finish()
-    for stage in scatter[2:]:
-        stage.start()
-        stage.finish()
+    scatter[2].finish()
+    scatter[3].start()
+    scatter[3].finish()
     for stage in gather:
         stage.start()
         stage.finish()

time: 173 us -> 171 us (0.988)
  Pallas kernels: 118 us -> 116 us
    pallas_call x1, Pallas kernels: 33.6 us -> 31.8 us  [sum_over_all(): pl.pallas_call(functools.partial(sum_kernel, sizes), out_shape=jax.ShapeD...]
where the time goes in v5:
time: 171 us; the launch traced here: 170 us
  Pallas kernels  116 us (68%)
  local copies, waits for them, and re-layouts  27 us (16%)
  matrix products  21.5 us (13%)
  other arithmetic  5.24 us (3%)
    pallas_call x1, Pallas kernels, smooth(): pl.pallas_call(functools.partial(smooth_kernel, sizes, depth, frames, own...  72.1 us
    pallas_call x1, Pallas kernels, sum_over_all(): pl.pallas_call(functools.partial(sum_kernel, sizes), out_shape=jax.ShapeD...  31.8 us
    dot_general x1, matrix products, body(): lax.dot_general(turned, stacked, (((0,), (0,)), ((), ())), preferred_elem...  11.6 us
    pallas_call x1, Pallas kernels, exchange(): pl.pallas_call(functools.partial(exchange_kernel, total, groups, summed),...  11.6 us
    dot_general x1, matrix products, body(): lax.dot_general(subspace, jnp.concatenate(spread), across, preferred_elem...  8.32 us
    pad x1, local copies, waits for them, and re-layouts, body(): jnp.pad(raw_frames.transpose(1, 0, 2), ((0, 0), (0, 0), (LEFT, SPAN - WID...  7.52 us
    convert_element_type x1, local copies, waits for them, and re-layouts, body(): basis_part = lax.dot_general(subspace, jnp.concatenate(spread), across, p...  5.99 us
    unnamed x20, local copies, waits for them, and re-layouts  5.82 us

profile of v5, /device:TPU:0, one launch (start us, length us, event | category | flops | bytes accessed | tf_op | source)
XLA Modules:
  0.0 170.2 jit_solution(18108440906265934048)
XLA Ops:
  0.6 0.0 copy-start.5
  0.7 0.8 slice_reduce_fusion
  1.5 0.5 pad_bitcast_fusion.x_ref
  2.0 11.6 %shard_map.77 = s32[32,1,128]{2,1,0:T(1,128)} custom-call(s32[1,128]{1,0:T(1,128)} %pad_bitcast_fusion.x_ref), custom_call_target="tpu_custom_call" | custom-call | tf_op jit(solution)/shard_map/pallas_call | solution.py:101
  13.6 0.8 subtract_reduce_fusion
  14.3 0.1 sub.32
  14.4 0.1 slice_bitcast_fusion
  14.5 0.1 fusion.6
  14.6 0.1 fusion.3
  14.7 0.8 add.117.r_ref
  15.5 0.7 fusion.5
  16.3 0.8 select_n.49.z_ref
  17.1 0.0 copy-start
  17.1 2.7 %fusion.8 = (bf16[182,1792]{1,0:T(8,128)(2,1)S(1)}, bf16[182,1792]{1,0:T(8,128)(2,1)S(1)}, bf16[182,1792]{1,0:T(8,128)(2,1)S(1)}, bf16[182,1792]{1,0:T(8,128)(2,1)S(1)}, bf16[182,1792]{1,0:T(8,128)(2,1)S(1)}) fusion(bf16[1200,1792]{1,0:T(8,128)(2,1)} %param.8), kind=kLoop, calls=%fused_computation.49 | loop fusion | bytes 6522880 | tf_op jit(solution)/shard_map/slice | solution.py:508
  19.8 0.0 copy-done.5
  19.8 0.5 copy-done
  20.3 0.2 select_dynamic-update-slice_fusion
  20.8 0.1 slice.52
  21.0 8.3 %convolution_convert_fusion = bf16[1536,1200]{0,1:T(8,128)(2,1)} fusion(bf16[1536,1792]{1,0:T(8,128)(2,1)S(1)} %broadcast_dynamic-update-slice_fusion, bf16[1200,1792]{1,0:T(8,128)(2,1)S(1)} %copy-done), kind=kOutput, calls=%fused_computation | convolution fusion | flops 6607872000 | bytes 13492224 | tf_op jit(solution)/shard_map/dot_general | solution.py:510
  29.3 6.0 %copy.14 = bf16[1536,1200]{1,0:T(8,128)(2,1)} copy(bf16[1536,1200]{0,1:T(8,128)(2,1)} %convolution_convert_fusion) | data formatting | bytes 7372800 | tf_op jit(solution)/shard_map/convert_element_type | solution.py:512
  35.3 7.5 %pad.39 = bf16[12,32,11520]{2,1,0:T(8,128)(2,1)} pad(bf16[12,32,10752]{2,1,0:T(8,128)(2,1)} %bitcast.28, bf16[]{:T(256)} %constant.82.clone.1), padding=0_0x0_0x384_384 | pad | bytes 17104898 | tf_op jit(solution)/shard_map/jit(_pad)/pad | solution.py:515
  42.8 72.1 %shard_map.78 = (bf16[256,1792]{1,0:T(8,128)(2,1)}, bf16[2,2,48,1200]{3,2,1,0:T(8,128)(2,1)}) custom-call(f32[1176]{0:T(1024)} %select_n.49.z_ref, s32[1176]{0:T(1024)} %add.117.r_ref, bf16[384,11520]{1,0:T(8,128)(2,1)} %bitcast.25, bf16[3,1024,256]{2,1,0:T(8,128)(2,1)} %constant.97.clone.w_ref, bf16[4,2,2,2,48,1200]{5,4,3,2,1,0:T(8,128)(2,1)} %bitcast.27), custom_call_target="tpu_custom_call" | custom-call | tf_op jit(solution)/shard_map/pallas_call | solution.py:411
  114.9 0.0 copy-start.3
  114.9 2.6 %constant_dynamic-update-slice_fusion.1 = bf16[1456,1792]{1,0:T(8,128)(2,1)S(1)} fusion(bf16[1200,1792]{1,0:T(8,128)(2,1)} %param.8), kind=kLoop, calls=%fused_computation.26 | loop fusion | bytes 8601600
  117.5 0.0 copy-done.3
  117.5 0.1 constant_dynamic-update-slice_fusion
  117.6 0.0 copy-start.2
  117.6 2.3 %copy-done.2 = bf16[1456,1792]{1,0:T(8,128)(2,1)} copy-done((bf16[1456,1792]{1,0:T(8,128)(2,1)}, bf16[1456,1792]{1,0:T(8,128)(2,1)S(1)}, u32[]{:S(2)}) %copy-start.2) | copy-done | bytes 5218328
  119.9 1.6 convolution_convert_fusion.2
  121.5 1.2 copy.15
  122.6 31.8 %shard_map.79 = bf16[1,8,2,2,8,1456]{5,4,3,2,1,0:T(8,128)(2,1)} custom-call(bf16[1,8,2,2,8,1456]{5,4,3,2,1,0:T(8,128)(2,1)} %bitcast.29), custom_call_target="tpu_custom_call" | custom-call | tf_op jit(solution)/shard_map/pallas_call | solution.py:455
  154.5 1.5 select_reduce_fusion
  156.0 0.1 reduce_sum.21
  156.1 0.1 reduce_sum.22
  156.3 0.1 broadcast_bitcast_fusion
  156.3 0.1 concatenate.48
  156.4 0.0 copy-start.1
  156.4 0.0 copy-start.4
  156.4 11.6 %convolution_convert_fusion.1 = bf16[1200,1792]{1,0:T(8,128)(2,1)} fusion(bf16[1456,1792]{1,0:T(8,128)(2,1)} %copy-done.2, bf16[1456,1200]{0,1:T(8,128)(2,1)} %param.9, f32[1456]{0:T(1024)S(1)} %concatenate.48), kind=kOutput, calls=%fused_computation.1 | convolution fusion | flops 6269357056 | bytes 13019328 | tf_op jit(solution)/shard_map/dot_general | solution.py:539
  168.0 0.0 copy-done.1
  168.0 0.1 slice.57
  168.1 0.0 copy-done.4
  168.1 0.2 fusion.2
  168.3 0.2 bitcast_convert_fusion
  168.6 0.1 constant_dynamic-slice_fusion
  168.7 0.1 copy.17
  168.8 0.1 pad_dynamic-slice_fusion.1
  168.9 1.2 fusion.1
  (11 shorter events, 0.4 us)
Async XLA Ops:
  0.6 19.1 %copy-start.5 = (pred[192]{0:T(512)(128)(4,1)S(1)}, pred[192]{0:T(512)(128)(4,1)}, u32[]{:S(2)}) copy-start(pred[192]{0:T(512)(128)(4,1)} %constant.83.clone.1) | copy-start | bytes 580
  17.1 3.2 %copy-start = (bf16[1200,1792]{1,0:T(8,128)(2,1)S(1)}, bf16[1200,1792]{1,0:T(8,128)(2,1)}, u32[]{:S(2)}) copy-start(bf16[1200,1792]{1,0:T(8,128)(2,1)} %param.8) | copy-start | bytes 12902404
  114.9 2.6 %copy-start.3 = (bf16[256,1792]{1,0:T(8,128)(2,1)S(1)}, bf16[256,1792]{1,0:T(8,128)(2,1)}, u32[]{:S(2)}) copy-start(bf16[256,1792]{1,0:T(8,128)(2,1)} %get-tuple-element.5) | copy-start | bytes 2752516
  117.6 2.3 %copy-start.2 = (bf16[1456,1792]{1,0:T(8,128)(2,1)}, bf16[1456,1792]{1,0:T(8,128)(2,1)S(1)}, u32[]{:S(2)}) copy-start(bf16[1456,1792]{1,0:T(8,128)(2,1)S(1)} %constant_dynamic-update-slice_fusion) | copy-start | bytes 15654916
  156.4 11.6 %copy-start.1 = (bf16[1,8,2,2,8,1456]{5,4,3,2,1,0:T(8,128)(2,1)S(1)}, bf16[1,8,2,2,8,1456]{5,4,3,2,1,0:T(8,128)(2,1)}, u32[]{:S(2)}) copy-start(bf16[1,8,2,2,8,1456]{5,4,3,2,1,0:T(8,128)(2,1)} %shard_map.79) | copy-start | bytes 2236420
  156.4 11.7 %copy-start.4 = (bf16[2,2,48,1200]{3,2,1,0:T(8,128)(2,1)S(1)}, bf16[2,2,48,1200]{3,2,1,0:T(8,128)(2,1)}, u32[]{:S(2)}) copy-start(bf16[2,2,48,1200]{3,2,1,0:T(8,128)(2,1)} %get-tuple-element.4) | copy-start | bytes 1382404
